TPU v7x, 32 devices: a whole 2x2x4 slice. The times are simulated.
32 devices in a mesh: ctx: 8 (over z, y), fsdp: 4 (over x, core).
Axes of the slice: x: 2, y: 2, z: 4, core: 2. Of those that a mesh axis runs over, the one named last changes fastest.
Arguments:
- hidden: bfloat16 [4096, 4096], P('ctx', 'fsdp'), may hold values from -6 to 6
- w_in: bfloat16 [768, 4096], P('ctx', 'fsdp'), may hold values from -1.25 to 1.25
- decay: float32 [4, 4096], P(None, 'ctx'), may hold values from 0.999 to 1
- norm_gain: float32 [256], replicated, may hold values from 0.1 to 1.9
- w_out: bfloat16 [256, 4096], P('ctx', 'fsdp'), may hold values from -0.75 to 0.75
- grad_out: bfloat16 [4096, 4096], P('ctx', 'fsdp'), may hold values from -6 to 6
Outputs:
- grad_hidden: bfloat16 [4096, 4096], P('ctx', 'fsdp')
- grad_w_in: float32 [768, 4096], P('ctx', 'fsdp')
- grad_w_out: float32 [256, 4096], P('ctx', 'fsdp')
All inputs are finite; a program needn't handle non-finite values.
Results may differ from a plain program's by a relative error of at most 0.0075.
Values may be sent and summed in bfloat16 or wider, within the bound.
A program may use at most 128 MiB of HBM per device.

v0:
```python
import functools
import math

import jax
import jax.numpy as jnp
from jax import lax
from jax.experimental import pallas as pl
from jax.experimental.pallas import tpu as pltpu
from jax.sharding import PartitionSpec as P

D = 4096
H = 4
P_SIZE = 64
N = 128
HP = 256


highest = lax.Precision.HIGHEST
clip_output = 10.0


def prefix(x, axis, combine, identity):
    count, index = (lax.axis_size(axis), lax.axis_index(axis))
    everything = jax.tree.map(lambda part: lax.all_gather(part, axis), x)
    start = jax.tree.map(
        lambda part, zero: jnp.broadcast_to(jnp.asarray(zero, part.dtype), part.shape), x, identity
    )

    def step(k, before):
        reached = k < index
        new = combine(before, jax.tree.map(lambda part: part[k], everything))
        return jax.tree.map(lambda a, b: jnp.where(reached, a, b), new, before)

    return lax.fori_loop(0, count, step, start)


def entering(x, axis, join, neutral):
    count = lax.axis_size(axis)
    place = lax.axis_index(axis)
    ahead = count - 1 - place
    gathered = jax.tree.map(
        lambda a, kind: lax.all_gather(a.astype(kind), axis),
        x,
        jax.tree.map(lambda a: jnp.bfloat16 if a.dtype == jnp.float32 else a.dtype, x),
    )
    state = jax.tree.map(lambda a, e: jnp.zeros_like(a) + jnp.asarray(e, a.dtype), x, neutral)

    def one(step, state):
        source = count - 1 - step
        return join(
            state,
            jax.tree.map(
                lambda a, own: lax.dynamic_index_in_dim(a, source, 0, False).astype(own.dtype),
                gathered,
                x,
            ),
        )

    return lax.fori_loop(0, ahead, one, state)


def split_columns(projection):
    return (
        projection[:, :HP],
        projection[:, HP : 2 * HP],
        projection[:, 2 * HP : 2 * HP + N],
        projection[:, 2 * HP + N :],
    )


def intra_block(x_part, b_part, c_part, log_decay):
    length = x_part.shape[0]
    cum_decay = jnp.cumsum(log_decay, axis=1)
    x_heads = x_part.reshape(length, H, P_SIZE)
    causal = jnp.arange(length)[:, None] >= jnp.arange(length)[None, :]
    gaps = jnp.where(causal[None], cum_decay[:, :, None] - cum_decay[:, None, :], 0.0)
    weights = jnp.where(causal[None], jnp.exp(gaps), 0.0)
    scores = jnp.dot(c_part, b_part.T, precision=highest)
    mixed = weights * scores[None]
    y_intra = jnp.einsum("hts,shp->thp", mixed, x_heads, precision=highest).reshape(
        length, H * P_SIZE
    )
    tail = jnp.exp(cum_decay[:, -1:] - cum_decay)
    weighted = x_heads * tail.T[:, :, None]
    state_part = jnp.einsum("shp,sn->hpn", weighted, b_part, precision=highest)
    return (y_intra, state_part, cum_decay)


def finish_block(gate_part, y_intra, c_part, start_state, cum_decay, norm_gain):
    length = c_part.shape[0]
    carried = jnp.einsum("hpn,tn->thp", start_state, c_part, precision=highest)
    carried = carried * jnp.exp(cum_decay).T[:, :, None]
    y_full = y_intra + carried.reshape(length, H * P_SIZE)
    gated = y_full * jax.nn.silu(gate_part)
    factor = lax.rsqrt(jnp.mean(gated * gated, axis=-1, keepdims=True) + 1e-05)
    return gated * factor * norm_gain


def carry_states(earlier, later):
    return (earlier[0] * later[0], later[0] * earlier[1] + later[1])


def carry_adjoint(earlier, later):
    return (earlier[0] * later[0], later[1] + later[0] * earlier[1])


def local(hidden, w_in, decay, norm_gain, w_out, grad_out):
    clip_input = math.sqrt(D)
    tok_rows = hidden.shape[0]
    root_tokens = math.sqrt(tok_rows * lax.axis_size("ctx"))
    contract_last = (((1,), (1,)), ((), ()))
    contract_first = (((0,), (0,)), ((), ()))
    partial_proj = lax.dot_general(
        hidden,
        lax.all_gather(w_in, "ctx", axis=0, tiled=True),
        contract_last,
        preferred_element_type=jnp.float32,
    )
    slab_out = lax.all_gather(w_out, "ctx", axis=0, tiled=True)
    partial_grad = lax.dot_general(
        grad_out, slab_out, contract_last, preferred_element_type=jnp.float32
    )
    projection, grad_normed = lax.psum((partial_proj, partial_grad), "fsdp")
    log_decay = jnp.log(decay)
    gate_part, x_part, b_part, c_part = split_columns(projection)

    def intra_only(x_value, b_value, c_value):
        return intra_block(x_value, b_value, c_value, log_decay)

    (y_intra, state_part, cum_decay), intra_pull = jax.vjp(intra_only, x_part, b_part, c_part)
    decay_total = jnp.exp(cum_decay[:, -1])[:, None, None]
    identity = (jnp.ones_like(decay_total), jnp.zeros_like(state_part))
    _, start_state = prefix((decay_total, state_part), "ctx", carry_states, identity)

    def finish_only(gate_value, intra_value, c_value, state_value):
        return finish_block(gate_value, intra_value, c_value, state_value, cum_decay, norm_gain)

    normed, finish_pull = jax.vjp(finish_only, gate_part, y_intra, c_part, start_state)
    grad_gate, grad_intra, grad_c_late, grad_start = finish_pull(grad_normed)
    _, grad_end = entering((decay_total, grad_start), "ctx", carry_adjoint, identity)
    grad_x, grad_b, grad_c_early = intra_pull((grad_intra, grad_end, jnp.zeros_like(cum_decay)))
    grad_projection = jnp.concatenate(
        [grad_gate, grad_x, grad_b, grad_c_early + grad_c_late], axis=1
    ).astype(jnp.bfloat16)
    columns = grad_projection
    grad_hidden = jnp.dot(
        columns, lax.all_gather(w_in, "ctx", axis=0, tiled=True), preferred_element_type=jnp.float32
    )
    columns = grad_projection
    raw_in = (
        lax.psum_scatter(
            lax.dot_general(columns, hidden, contract_first, preferred_element_type=jnp.float32),
            "ctx",
            scatter_dimension=0,
            tiled=True,
        )
        / root_tokens
    )
    weight_square = jnp.sum(jnp.square(w_in.astype(jnp.float32)), axis=1)
    weight_in, grad_in = lax.psum((weight_square, jnp.sum(raw_in * raw_in, axis=1)), "fsdp")
    factor_in = jnp.minimum(
        1.0,
        clip_input
        * jnp.maximum(jnp.sqrt(weight_in), 0.001)
        / jnp.maximum(jnp.sqrt(grad_in), 1e-06),
    )
    normed_rounded = normed.astype(jnp.bfloat16)
    weight_out = jnp.sqrt(jnp.sum(jnp.square(slab_out.astype(jnp.float32)), axis=0))
    raw_out = (
        lax.psum_scatter(
            lax.dot_general(
                normed_rounded, grad_out, contract_first, preferred_element_type=jnp.float32
            ),
            "ctx",
            scatter_dimension=0,
            tiled=True,
        )
        / root_tokens
    )
    grad_square = lax.psum(jnp.sum(raw_out * raw_out, axis=0), "ctx")
    factor_out = jnp.minimum(
        1.0,
        clip_output * jnp.maximum(weight_out, 0.001) / jnp.maximum(jnp.sqrt(grad_square), 1e-06),
    )
    return (
        grad_hidden.astype(jnp.bfloat16),
        raw_in * factor_in[:, None],
        raw_out * factor_out[None, :],
    )


NN = (((1,), (0,)), ((), ()))
NT = (((1,), (1,)), ((), ()))
TN = (((0,), (0,)), ((), ()))
MESH = pl.DeviceIdType.MESH
f32 = jnp.float32
bf16 = jnp.bfloat16
EPS = 1e-05


def split(a):
    hi = a.astype(bf16)
    return hi, (a - hi.astype(f32)).astype(bf16)


def dot1(a, b, dims):
    return lax.dot_general(a, b, dims, preferred_element_type=f32)


def dot3(a, b, dims):
    return dot1(a[0], b[0], dims) + (dot1(a[0], b[1], dims) + dot1(a[1], b[0], dims))


def transposed(pair):
    return pair[0].T, pair[1].T


def fused(
    n, fs, root_tokens, clip_input,
    hid_ref, win_ref, dec_ref, gain_ref, wout_ref, gout_ref,
    gh_ref, gwi_ref, gwo_ref,
    hidT, goutT, wi_all, wo_all, pT, buf, core_in, x_out, x_in, c_in, e_out, e_all,
    e_ref, st_out, st_all, s0_ref, ad_out, ad_all, g_ref,
    ro, ob1, ob1r, ob2, ob2r, gp, ri, ib1, ib1r, ib2, ib2r,
    nin_out, nin_all, nout_out, nout_all,
    g_send, g_recv, p_send, p_recv, s_send, s_recv, o_send, o_recv, i_send, i_recv,
    n_send, n_recv, tmp,
):
    c = lax.axis_index("ctx")
    f = lax.axis_index("fsdp")
    outer = n // 2
    z, y = c // 2, lax.rem(c, 2)
    yn = c + 1 - 2 * y
    core = lax.rem(f, 2)
    fcore = f + 1 - 2 * core
    fx = lax.rem(f + fs // 2, fs)
    rows_in, d = win_ref.shape
    rows_out = wout_ref.shape[0]
    tok = hid_ref.shape[0]
    cin, hp = rows_in * n, rows_out * n
    nst = (cin - 2 * hp) // 2
    hpf = hp // fs

    def copy(src, dst, ssem, rsem, dev):
        return pltpu.make_async_remote_copy(
            src_ref=src, dst_ref=dst, send_sem=ssem, recv_sem=rsem,
            device_id=dev, device_id_type=MESH)

    sent = []

    def go(*args, when=None):
        if when is None:
            copy(*args).start()
        else:
            pl.when(when)(lambda: copy(*args).start())
        sent.append((when, args))

    def arrive(*args, when=None):
        if when is None:
            copy(*args).wait_recv()
        else:
            pl.when(when)(lambda: copy(*args).wait_recv())

    barrier = pltpu.get_barrier_semaphore()
    for k in range(1, n):
        pl.semaphore_signal(barrier, inc=1, device_id=(lax.rem(c + k, n), f), device_id_type=MESH)
    for k in range(1, fs):
        pl.semaphore_signal(barrier, inc=1, device_id=(c, lax.rem(f + k, fs)), device_id_type=MESH)
    pl.semaphore_wait(barrier, n + fs - 2)

    both = ((win_ref, wi_all), (wout_ref, wo_all))
    up = jnp.minimum(z + 1, outer - 1) * 2 + y
    down = jnp.maximum(z - 1, 0) * 2 + y
    order = [1, outer - 1] + list(range(2, outer - 1))
    for a, (src, dst) in enumerate(both):
        go(src, dst.at[c], g_send.at[0, a, c], g_recv.at[a, c], (up, f), when=z < outer - 1)
        go(src, dst.at[c], g_send.at[1, a, c], g_recv.at[a, c], (down, f), when=z > 0)
        go(src, dst.at[c], g_send.at[2, a, c], g_recv.at[a, c], (yn, f))
    wi_all[c] = win_ref[...]
    wo_all[c] = wout_ref[...]
    hidT[...] = hid_ref[...].T
    goutT[...] = gout_ref[...].T

    decay = dec_ref[...]
    lane = lax.broadcasted_iota(jnp.int32, decay.shape, 1)
    shift = 1
    while shift < tok:
        decay = decay * jnp.where(lane >= shift, pltpu.roll(decay, shift, 1), 1.0)
        shift *= 2
    heads = decay.shape[0]
    for h in range(heads):
        e_ref[h * (hp // heads) : (h + 1) * (hp // heads), :] = jnp.broadcast_to(
            decay[h : h + 1], (hp // heads, tok))

    e_out[...] = jnp.broadcast_to(
        e_ref[pl.ds(pl.multiple_of(f * hpf, 8), 8), tok - 128 : tok][:, 127:128], (8, nst))
    e_all[c] = e_out[...]
    for k in range(1, n):
        go(e_out, e_all.at[c], s_send.at[4, k], s_recv.at[4, c], (lax.rem(c + k, n), f))

    hi, ho = rows_in // 2, rows_out // 2
    half = hi + ho
    mine = pl.ds(pl.multiple_of(core * half, 8), half)
    other = pl.ds(pl.multiple_of((1 - core) * half, 8), half)

    def place(s, which, value):
        pT[pl.ds(pl.multiple_of(s * rows_in + which * hi, 8), hi), :] = value[:hi]
        pT[pl.ds(pl.multiple_of(cin + s * rows_out + which * ho, 8), ho), :] = value[hi:]

    def to_pair(s):
        return (buf.at[s, other], core_in.at[s], p_send.at[0, s], p_recv.at[0, s], (c, fcore))

    def across(s):
        return (x_out.at[s], x_in.at[s], p_send.at[1, s], p_recv.at[1, s], (c, fx))

    def back(s):
        return (buf.at[s, mine], c_in.at[s], p_send.at[2, s], p_recv.at[2, s], (c, fcore))

    def project(s):
        left = dot1(wi_all[s], hidT[...], NN)
        right = dot1(wo_all[s], goutT[...], NN)
        buf[s, :hi] = left[:hi]
        buf[s, hi:half] = right[:ho]
        buf[s, half : half + hi] = left[hi:]
        buf[s, half + hi :] = right[ho:]
        copy(*to_pair(s)).start()

    def pair_sum(s):
        copy(*to_pair(s)).wait_recv()
        total = buf[s, mine] + core_in[s]
        buf[s, mine] = total
        x_out[s] = total.astype(bf16)
        copy(*across(s)).start()

    def full_sum(s):
        copy(*across(s)).wait_recv()
        total = buf[s, mine] + x_in[s].astype(f32)
        buf[s, mine] = total
        copy(*back(s)).start()
        place(s, core, total)

    def collect(s):
        copy(*back(s)).wait_recv()
        place(s, 1 - core, c_in[s])

    def landed(s, fwd, across_pair):
        for a, (src, dst) in enumerate(both):
            copy(dst.at[s], dst.at[s], g_send.at[2, a, s], g_recv.at[a, s], (yn, f)).wait_recv()
            if fwd is not None:
                has, to, way = fwd
                pl.when(has)(lambda: copy(
                    dst.at[s], dst.at[s], g_send.at[way, a, s], g_recv.at[a, s], (to, f)).start())
            if across_pair:
                copy(dst.at[s], dst.at[s], g_send.at[2, a, s], g_recv.at[a, s], (yn, f)).start()

    def row(k, way):
        there = z - k if way == 0 else z + k
        has = there >= 0 if way == 0 else there < outer
        q = jnp.maximum(there, 0) if way == 0 else jnp.minimum(there, outer - 1)
        fwd = (z < outer - 1, up, 0) if way == 0 else (z > 0, down, 1)
        return has, q, fwd

    events = [(None, c, None, False, False)]
    later = [(None, z * 2 + 1 - y, None, True, False)]
    for k in range(1, outer):
        for way in (0, 1):
            has, q, fwd = row(k, way)
            events.append((has, q * 2 + y, fwd, True, True))
        events.extend(later)
        later = []
        for way in (0, 1):
            has, q, fwd = row(k, way)
            later.append((has, q * 2 + 1 - y, None, True, False))
    events.extend(later)

    def under(has, fn, *args):
        if has is None:
            fn(*args)
        else:
            pl.when(has)(lambda: fn(*args))

    def take(s, fwd, wait, across_pair):
        if wait:
            landed(s, fwd, across_pair)
        project(s)

    def release(s, fwd, across_pair):
        for args in (to_pair(s), across(s), back(s)):
            copy(*args).wait_send()
        for a, (src, dst) in enumerate(both):
            def there(way, to):
                copy(dst.at[s], dst.at[s], g_send.at[way, a, s], g_recv.at[a, s],
                     (to, f)).wait_send()
            if fwd is not None:
                under(fwd[0], there, fwd[2], fwd[1])
            if across_pair:
                there(2, yn)

    total_events = len(events)
    for i in range(total_events + 5):
        if i < total_events:
            has, s, fwd, wait, across_pair = events[i]
            under(has, take, s, fwd, wait, across_pair)
        for lag, fn in ((1, pair_sum), (3, full_sum), (5, collect)):
            if 0 <= i - lag < total_events:
                under(events[i - lag][0], fn, events[i - lag][1])

    e = e_ref[...]
    einv = 1.0 / e
    eend = e[:, tok - 1 : tok]
    gate = pT[:hp, :]
    xs = pT[hp : 2 * hp, :] * einv
    bT = pT[2 * hp : 2 * hp + nst, :]
    cT = pT[2 * hp + nst : cin, :]
    xs2, b2, c2 = split(xs), split(bT), split(cT)
    tmp[...] = dot3(xs2, b2, NT) * eend
    own = pl.ds(pl.multiple_of(f * hpf, 8), hpf)
    st_out[...] = tmp[own, :]
    for k in range(n - 1, 0, -1):
        go(st_out, st_all.at[c], s_send.at[0, k], s_recv.at[0, c],
           (jnp.minimum(c + k, n - 1), f), when=c + k < n)

    upper = lax.broadcasted_iota(jnp.int32, (tok, tok), 0) <= lax.broadcasted_iota(
        jnp.int32, (tok, tok), 1)
    scores2 = split(jnp.where(upper, dot3(transposed(b2), c2, NN), 0.0))
    y_in = dot3(xs2, scores2, NN)
    sig = 1.0 / (1.0 + jnp.exp(-gate))
    silu = gate * sig

    for k in range(1, n):
        s = lax.rem(c + n - k, n)
        arrive(e_out, e_all.at[s], s_send.at[4, k], s_recv.at[4, s], (s, f))
        s = jnp.maximum(c - k, 0)
        arrive(st_out, st_all.at[s], s_send.at[0, k], s_recv.at[0, s], (s, f), when=c - k >= 0)
    state = jnp.zeros((hpf, nst), f32)
    for k in range(n - 1):
        new = e_all[k, 0:1, :] * state + st_all[k]
        state = jnp.where(k < c, new, state)
    s0_ref[own, :] = state
    for k in range(1, fs):
        go(s0_ref.at[own], s0_ref.at[own], s_send.at[1, k], s_recv.at[1, f], (c, lax.rem(f + k, fs)))
    for k in range(1, fs):
        p = lax.rem(f + fs - k, fs)
        rows = pl.ds(pl.multiple_of(p * hpf, 8), hpf)
        copy(s0_ref.at[rows], s0_ref.at[rows], s_send.at[1, k], s_recv.at[1, p], (c, p)).wait_recv()
    s02 = split(s0_ref[...])
    yT = (y_in + dot3(s02, c2, NN)) * e

    gain = gain_ref[...]
    gated = yT * silu
    r = lax.rsqrt(jnp.mean(gated * gated, axis=0, keepdims=True) + EPS)
    normed = (gated * r * gain).astype(bf16)
    u = pT[cin:, :] * gain
    dgated = r * u - gated * (r * r * r * jnp.mean(u * gated, axis=0, keepdims=True))
    dys2 = split(dgated * silu * e)
    tmp[...] = dot3(dys2, c2, NT)
    ad_out[...] = tmp[own, :].astype(bf16)
    for k in range(n - 1, 0, -1):
        go(ad_out, ad_all.at[c], s_send.at[2, k], s_recv.at[2, c],
           (jnp.maximum(c - k, 0), f), when=c - k >= 0)
    gp[:hp, :] = (dgated * yT * (sig * (1.0 + gate * (1.0 - sig)))).astype(bf16)

    ro[...] = dot1(normed, gout_ref[...], NN)
    for q in range(outer):
        at = pl.ds(pl.multiple_of((q * 2 + 1 - y) * rows_out, 8), rows_out)
        ob1[q] = ro[at, :].astype(bf16)
    go(ob1, ob1r, o_send.at[0], o_recv.at[0], (yn, f))

    dscores = jnp.where(upper, dot1(xs2[0].T, dys2[0], NN), 0.0).astype(bf16)
    gp[2 * hp + nst :, :] = (dot1(b2[0], dscores, NN) + dot3(transposed(s02), dys2, NN)).astype(bf16)
    db = dot1(c2[0], dscores, NT)
    dxs = dot1(dys2[0], scores2[0], NT)

    copy(ob1, ob1r, o_send.at[0], o_recv.at[0], (yn, f)).wait_recv()
    for q in range(outer):
        at = pl.ds(pl.multiple_of((q * 2 + y) * rows_out, 8), rows_out)
        total = ro[at, :] + ob1r[q].astype(f32)
        ro[at, :] = total
        ob2[q] = total.astype(bf16)

    for k in range(1, n):
        s = jnp.minimum(c + k, n - 1)
        arrive(ad_out, ad_all.at[s], s_send.at[2, k], s_recv.at[2, s], (s, f), when=c + k < n)
    adj = jnp.zeros((hpf, nst), f32)
    for k in range(n - 1, 0, -1):
        new = e_all[k, 0:1, :] * adj + ad_all[k].astype(f32)
        adj = jnp.where(k > c, new, adj)
    g_ref[own, :] = adj
    for k in range(1, fs):
        go(g_ref.at[own], g_ref.at[own], s_send.at[3, k], s_recv.at[3, f], (c, lax.rem(f + k, fs)))
    for k in range(1, outer):
        q = lax.rem(z + k, outer)
        go(ob2.at[q], ob2r.at[z], o_send.at[k], o_recv.at[1 + z], (q * 2 + y, f))
    for k in range(1, fs):
        p = lax.rem(f + fs - k, fs)
        rows = pl.ds(pl.multiple_of(p * hpf, 8), hpf)
        copy(g_ref.at[rows], g_ref.at[rows], s_send.at[3, k], s_recv.at[3, p], (c, p)).wait_recv()
    g2 = split(g_ref[...] * eend)
    gp[hp : 2 * hp, :] = ((dxs + dot3(g2, b2, NN)) * einv).astype(bf16)
    gp[2 * hp : 2 * hp + nst, :] = (db + dot3(transposed(g2), xs2, NN)).astype(bf16)

    def rows_of(s):
        return pl.ds(pl.multiple_of(s * rows_in, 16), rows_in)

    far = order[::-1] + [0]
    for i, k in enumerate(far):
        q = lax.rem(z + k, outer)
        ib1[i] = dot1(gp[rows_of(q * 2 + 1 - y), :], hid_ref[...], NN).astype(bf16)
        go(ib1.at[i], ib1r.at[i], i_send.at[0, i], i_recv.at[0, i], (yn, f))
    for i, k in enumerate(far):
        q = lax.rem(z + k, outer)
        part = dot1(gp[rows_of(q * 2 + y), :], hid_ref[...], NN)
        copy(ib1.at[i], ib1r.at[i], i_send.at[0, i], i_recv.at[0, i], (yn, f)).wait_recv()
        part = part + ib1r[i].astype(f32)
        if k:
            ib2[i] = part.astype(bf16)
            go(ib2.at[i], ib2r.at[z], i_send.at[1, i], i_recv.at[1, z], (q * 2 + y, f))
        else:
            ri[...] = part

    acc = ro[pl.ds(pl.multiple_of(c * rows_out, 8), rows_out), :]
    for k in range(1, outer):
        q = lax.rem(z + k, outer)
        copy(ob2.at[q], ob2r.at[q], o_send.at[k], o_recv.at[1 + q], (q * 2 + y, f)).wait_recv()
        acc = acc + ob2r[q].astype(f32)
    acc = acc * (1.0 / root_tokens)
    ro[:rows_out, :] = acc
    nout_out[...] = jnp.broadcast_to(jnp.sum(acc * acc, axis=0, keepdims=True), (8, d))
    for k in range(1, n):
        go(nout_out, nout_all.at[c], n_send.at[0, k], n_recv.at[0, c], (lax.rem(c + k, n), f))
    nout_all[c] = nout_out[...]

    gpt = gp[...].T
    wi = wi_all[...].reshape(cin, d)
    gh_ref[...] = dot1(gpt, wi, NN).astype(bf16)

    weight = jnp.zeros((1, d), f32)
    for s in range(n):
        w = wo_all[s].astype(f32)
        weight = weight + jnp.sum(w * w, axis=0, keepdims=True)
    w = win_ref[...].astype(f32)
    weight_in = jnp.sum(w * w, axis=1, keepdims=True)

    acc = ri[...]
    for k in range(1, outer):
        q = lax.rem(z + k, outer)
        copy(ib2.at[0], ib2r.at[q], i_send.at[1, 0], i_recv.at[1, q], (q * 2 + y, f)).wait_recv()
        acc = acc + ib2r[q].astype(f32)
    acc = acc * (1.0 / root_tokens)
    ri[...] = acc
    at = lax.broadcasted_iota(jnp.int32, (rows_in, 128), 1)
    nin_out[...] = jnp.where(at < 64, jnp.sum(acc * acc, axis=1, keepdims=True), weight_in)
    for k in range(1, fs):
        go(nin_out, nin_all.at[f], n_send.at[1, k], n_recv.at[1, f], (c, lax.rem(f + k, fs)))
    nin_all[f] = nin_out[...]

    grad_square = nout_all[c, 0:1, :]
    for k in range(1, n):
        s = lax.rem(c + n - k, n)
        copy(nout_out, nout_all.at[s], n_send.at[0, k], n_recv.at[0, s], (s, f)).wait_recv()
        grad_square = grad_square + nout_all[s, 0:1, :]
    factor = jnp.minimum(1.0, clip_output * jnp.maximum(jnp.sqrt(weight), 0.001)
                         / jnp.maximum(jnp.sqrt(grad_square), 1e-06))
    gwo_ref[...] = ro[:rows_out, :] * factor

    square = nin_all[f]
    for k in range(1, fs):
        p = lax.rem(f + fs - k, fs)
        copy(nin_out, nin_all.at[p], n_send.at[1, k], n_recv.at[1, p], (c, p)).wait_recv()
        square = square + nin_all[p]
    root = jnp.sqrt(square)
    factor = jnp.minimum(1.0, clip_input * jnp.maximum(root[:, 64:65], 0.001)
                         / jnp.maximum(root[:, 0:1], 1e-06))
    gwi_ref[...] = ri[...] * factor
    for has, args in sent:
        under(has, lambda args: copy(*args).wait_send(), args)
    for has, s, fwd, wait, across_pair in events:
        under(has, release, s, fwd, across_pair)


def one_kernel(n, fs, hidden, w_in, decay, norm_gain, w_out, grad_out):
    tok, d = hidden.shape
    rows_in, rows_out = w_in.shape[0], w_out.shape[0]
    cin, hp = rows_in * n, rows_out * n
    nst = (cin - 2 * hp) // 2
    hpf, outer = hp // fs, n // 2
    half = (rows_in + rows_out) // 2
    V = pltpu.VMEM
    dma = pltpu.SemaphoreType.DMA
    scratch = [
        V((d, tok), bf16), V((d, tok), bf16), V((n, rows_in, d), bf16), V((n, rows_out, d), bf16),
        V((cin + hp, tok), f32), V((n, 2 * half, tok), f32), V((n, half, tok), f32),
        V((n, half, tok), bf16), V((n, half, tok), bf16), V((n, half, tok), f32),
        V((8, nst), f32), V((n, 8, nst), f32),
        V((hp, tok), f32), V((hpf, nst), f32), V((n, hpf, nst), f32), V((hp, nst), f32),
        V((hpf, nst), bf16), V((n, hpf, nst), bf16), V((hp, nst), f32),
        V((hp, d), f32), V((outer, rows_out, d), bf16), V((outer, rows_out, d), bf16),
        V((outer, rows_out, d), bf16), V((outer, rows_out, d), bf16),
        V((cin, tok), bf16), V((rows_in, d), f32),
        V((outer, rows_in, d), bf16), V((outer, rows_in, d), bf16),
        V((outer, rows_in, d), bf16), V((outer, rows_in, d), bf16),
        V((rows_in, 128), f32), V((fs, rows_in, 128), f32), V((8, d), f32), V((n, 8, d), f32),
        dma((3, 2, n)), dma((2, n)), dma((3, n)), dma((3, n)), dma((5, n)), dma((5, n)),
        dma((1 + outer,)), dma((1 + outer,)), dma((2, outer)), dma((2, outer)),
        dma((2, n)), dma((2, n)), V((hp, nst), f32),
    ]
    vm = pl.BlockSpec(memory_space=pltpu.VMEM)
    return pl.pallas_call(
        functools.partial(fused, n, fs, math.sqrt(tok * n), math.sqrt(d * fs)),
        out_shape=(
            jax.ShapeDtypeStruct((tok, d), bf16),
            jax.ShapeDtypeStruct((rows_in, d), f32),
            jax.ShapeDtypeStruct((rows_out, d), f32),
        ),
        in_specs=[vm] * 6,
        out_specs=(vm, vm, vm),
        scratch_shapes=scratch,
        compiler_params=pltpu.CompilerParams(
            collective_id=0, has_side_effects=True, vmem_limit_bytes=60 * 1024 * 1024),
    )(hidden, w_in, decay, norm_gain[:, None], w_out, grad_out)


def solution(mesh):
    n, fs = mesh.shape["ctx"], mesh.shape["fsdp"]

    def body(hidden, w_in, decay, norm_gain, w_out, grad_out):
        whole_tiles = w_in.shape[0] % 16 == 0 and w_out.shape[0] % 16 == 0
        if whole_tiles and fs == decay.shape[0] and fs % 2 == 0 and n % 2 == 0 and n >= 4:
            return one_kernel(n, fs, hidden, w_in, decay, norm_gain, w_out, grad_out)
        return local(hidden, w_in, decay, norm_gain, w_out, grad_out)

    return jax.shard_map(
        body,
        mesh=mesh,
        in_specs=(
            P("ctx", "fsdp"),
            P("ctx", "fsdp"),
            P(None, "ctx"),
            P(),
            P("ctx", "fsdp"),
            P("ctx", "fsdp"),
        ),
        out_specs=(P("ctx", "fsdp"), P("ctx", "fsdp"), P("ctx", "fsdp")),
        check_vma=False,
    )
```

profile of v0, /device:TPU:0, one launch (start us, length us, event | category | flops | bytes accessed | tf_op | source)
XLA Modules:
  0.0 105.6 jit_solution(10499435448291487900)
XLA Ops:
  0.6 0.0 copy-start.2
  0.6 0.7 copy-done.2
  1.3 0.8 copy.9.gain_ref
  2.1 99.4 %shard_map.85 = (bf16[512,1024]{1,0:T(8,128)(2,1)}, f32[96,1024]{1,0:T(8,128)}, f32[32,1024]{1,0:T(8,128)}) custom-call(bf16[512,1024]{1,0:T(8,128)(2,1)} %hid_ref.1, bf16[96,1024]{1,0:T(8,128)(2,1)} %win_ref.1, f32[4,512]{1,0:T(4,128)} %dec_ref.1, f32[256,1]{1,0:T(8,128)} %copy.9.gain_ref, bf16[32,1024]{1,0:T(8,128)(2,1)} %wout_ref.1, ...), custom_call_target="tpu_custom_call" | custom-call | tf_op jit(solution)/shard_map/pallas_call | solution.py:608
  101.6 0.0 copy-start
  101.6 2.3 %copy.13 = bf16[512,1024]{1,0:T(8,128)(2,1)} copy(bf16[512,1024]{1,0:T(8,128)(2,1)} %get-tuple-element.6) | data formatting | bytes 2097152
  103.9 0.0 copy-done
  103.9 0.0 copy-start.1
  103.9 0.7 copy.14
  104.6 0.3 copy-done.1
  104.9 0.7 copy.15
Async XLA Ops:
  0.6 0.7 copy-start.2
  101.6 2.3 %copy-start = (f32[96,1024]{1,0:T(8,128)S(1)}, f32[96,1024]{1,0:T(8,128)}, u32[]{:S(2)}) copy-start(f32[96,1024]{1,0:T(8,128)} %get-tuple-element.7) | copy-start | bytes 1179652
  103.9 1.0 copy-start.1
where the time goes:
time: 107 us; the launch traced here: 106 us
  Pallas kernels  99.4 us (93%)
  local copies, waits for them, and re-layouts  5.47 us (5%)
    pallas_call x1, Pallas kernels, one_kernel(): pl.pallas_call(functools.partial(fused, n, fs, math.sqrt(tok * n), math.s...  99.4 us
    unnamed x9, local copies, waits for them, and re-layouts  4.67 us

commit v1 on v0

--- a/solution.py
+++ b/solution.py
@@ -217,14 +217,14 @@
 
 def fused(
     n, fs, root_tokens, clip_input,
-    hid_ref, win_ref, dec_ref, gain_ref, wout_ref, gout_ref,
-    gh_ref, gwi_ref, gwo_ref,
+    hid_any, win_ref, dec_any, gain_any, wout_ref, gout_any,
+    gh_any, gwi_any, gwo_any,
     hidT, goutT, wi_all, wo_all, pT, buf, core_in, x_out, x_in, c_in, e_out, e_all,
     e_ref, st_out, st_all, s0_ref, ad_out, ad_all, g_ref,
     ro, ob1, ob1r, ob2, ob2r, gp, ri, ib1, ib1r, ib2, ib2r,
     nin_out, nin_all, nout_out, nout_all,
     g_send, g_recv, p_send, p_recv, s_send, s_recv, o_send, o_recv, i_send, i_recv,
-    n_send, n_recv, tmp,
+    n_send, n_recv, tmp, hid_ref, gout_ref, dec_ref, gain_ref, gh_ref, gwi_ref, gwo_ref, l_sem,
 ):
     c = lax.axis_index("ctx")
     f = lax.axis_index("fsdp")
@@ -236,7 +236,7 @@
     fx = lax.rem(f + fs // 2, fs)
     rows_in, d = win_ref.shape
     rows_out = wout_ref.shape[0]
-    tok = hid_ref.shape[0]
+    tok = hid_any.shape[0]
     cin, hp = rows_in * n, rows_out * n
     nst = (cin - 2 * hp) // 2
     hpf = hp // fs
@@ -260,6 +260,15 @@
             copy(*args).wait_recv()
         else:
             pl.when(when)(lambda: copy(*args).wait_recv())
+
+    local = [
+        pltpu.make_async_copy(src, dst, l_sem.at[i])
+        for i, (src, dst) in enumerate((
+            (hid_any, hid_ref), (win_ref, wi_all.at[c]), (gout_any, gout_ref),
+            (wout_ref, wo_all.at[c]), (dec_any, dec_ref), (gain_any, gain_ref)))
+    ]
+    for each in local:
+        each.start()
 
     barrier = pltpu.get_barrier_semaphore()
     for k in range(1, n):
@@ -276,8 +285,8 @@
         go(src, dst.at[c], g_send.at[0, a, c], g_recv.at[a, c], (up, f), when=z < outer - 1)
         go(src, dst.at[c], g_send.at[1, a, c], g_recv.at[a, c], (down, f), when=z > 0)
         go(src, dst.at[c], g_send.at[2, a, c], g_recv.at[a, c], (yn, f))
-    wi_all[c] = win_ref[...]
-    wo_all[c] = wout_ref[...]
+    for each in local:
+        each.wait()
     hidT[...] = hid_ref[...].T
     goutT[...] = gout_ref[...].T
 
@@ -446,7 +455,7 @@
     s02 = split(s0_ref[...])
     yT = (y_in + dot3(s02, c2, NN)) * e
 
-    gain = gain_ref[...]
+    gain = jnp.broadcast_to(gain_ref[...].reshape(1, hp), (8, hp)).T[:, 0:1]
     gated = yT * silu
     r = lax.rsqrt(jnp.mean(gated * gated, axis=0, keepdims=True) + EPS)
     normed = (gated * r * gain).astype(bf16)
@@ -471,13 +480,6 @@
     db = dot1(c2[0], dscores, NT)
     dxs = dot1(dys2[0], scores2[0], NT)
 
-    copy(ob1, ob1r, o_send.at[0], o_recv.at[0], (yn, f)).wait_recv()
-    for q in range(outer):
-        at = pl.ds(pl.multiple_of((q * 2 + y) * rows_out, 8), rows_out)
-        total = ro[at, :] + ob1r[q].astype(f32)
-        ro[at, :] = total
-        ob2[q] = total.astype(bf16)
-
     for k in range(1, n):
         s = jnp.minimum(c + k, n - 1)
         arrive(ad_out, ad_all.at[s], s_send.at[2, k], s_recv.at[2, s], (s, f), when=c + k < n)
@@ -488,9 +490,6 @@
     g_ref[own, :] = adj
     for k in range(1, fs):
         go(g_ref.at[own], g_ref.at[own], s_send.at[3, k], s_recv.at[3, f], (c, lax.rem(f + k, fs)))
-    for k in range(1, outer):
-        q = lax.rem(z + k, outer)
-        go(ob2.at[q], ob2r.at[z], o_send.at[k], o_recv.at[1 + z], (q * 2 + y, f))
     for k in range(1, fs):
         p = lax.rem(f + fs - k, fs)
         rows = pl.ds(pl.multiple_of(p * hpf, 8), hpf)
@@ -498,6 +497,17 @@
     g2 = split(g_ref[...] * eend)
     gp[hp : 2 * hp, :] = ((dxs + dot3(g2, b2, NN)) * einv).astype(bf16)
     gp[2 * hp : 2 * hp + nst, :] = (db + dot3(transposed(g2), xs2, NN)).astype(bf16)
+
+    copy(ob1, ob1r, o_send.at[0], o_recv.at[0], (yn, f)).wait_recv()
+    for q in range(outer):
+        at = pl.ds(pl.multiple_of((q * 2 + y) * rows_out, 8), rows_out)
+        total = ro[at, :] + ob1r[q].astype(f32)
+        ro[at, :] = total
+        ob2[q] = total.astype(bf16)
+
+    for k in range(1, outer):
+        q = lax.rem(z + k, outer)
+        go(ob2.at[q], ob2r.at[z], o_send.at[k], o_recv.at[1 + z], (q * 2 + y, f))
 
     def rows_of(s):
         return pl.ds(pl.multiple_of(s * rows_in, 16), rows_in)
@@ -525,7 +535,7 @@
         acc = acc + ob2r[q].astype(f32)
     acc = acc * (1.0 / root_tokens)
     ro[:rows_out, :] = acc
-    nout_out[...] = jnp.broadcast_to(jnp.sum(acc * acc, axis=0, keepdims=True), (8, d))
+    nout_out[...] = jnp.sum(acc * acc, axis=0, keepdims=True).reshape(8, d // 8)
     for k in range(1, n):
         go(nout_out, nout_all.at[c], n_send.at[0, k], n_recv.at[0, c], (lax.rem(c + k, n), f))
     nout_all[c] = nout_out[...]
@@ -533,12 +543,14 @@
     gpt = gp[...].T
     wi = wi_all[...].reshape(cin, d)
     gh_ref[...] = dot1(gpt, wi, NN).astype(bf16)
+    put_gh = pltpu.make_async_copy(gh_ref, gh_any, l_sem.at[6])
+    put_gh.start()
 
     weight = jnp.zeros((1, d), f32)
     for s in range(n):
         w = wo_all[s].astype(f32)
         weight = weight + jnp.sum(w * w, axis=0, keepdims=True)
-    w = win_ref[...].astype(f32)
+    w = wi_all[c].astype(f32)
     weight_in = jnp.sum(w * w, axis=1, keepdims=True)
 
     acc = ri[...]
@@ -554,14 +566,17 @@
         go(nin_out, nin_all.at[f], n_send.at[1, k], n_recv.at[1, f], (c, lax.rem(f + k, fs)))
     nin_all[f] = nin_out[...]
 
-    grad_square = nout_all[c, 0:1, :]
+    grad_square = nout_all[c]
     for k in range(1, n):
         s = lax.rem(c + n - k, n)
         copy(nout_out, nout_all.at[s], n_send.at[0, k], n_recv.at[0, s], (s, f)).wait_recv()
-        grad_square = grad_square + nout_all[s, 0:1, :]
+        grad_square = grad_square + nout_all[s]
+    grad_square = grad_square.reshape(1, d)
     factor = jnp.minimum(1.0, clip_output * jnp.maximum(jnp.sqrt(weight), 0.001)
                          / jnp.maximum(jnp.sqrt(grad_square), 1e-06))
     gwo_ref[...] = ro[:rows_out, :] * factor
+    put_gwo = pltpu.make_async_copy(gwo_ref, gwo_any, l_sem.at[7])
+    put_gwo.start()
 
     square = nin_all[f]
     for k in range(1, fs):
@@ -572,10 +587,15 @@
     factor = jnp.minimum(1.0, clip_input * jnp.maximum(root[:, 64:65], 0.001)
                          / jnp.maximum(root[:, 0:1], 1e-06))
     gwi_ref[...] = ri[...] * factor
+    put_gwi = pltpu.make_async_copy(gwi_ref, gwi_any, l_sem.at[8])
+    put_gwi.start()
     for has, args in sent:
         under(has, lambda args: copy(*args).wait_send(), args)
     for has, s, fwd, wait, across_pair in events:
         under(has, release, s, fwd, across_pair)
+    put_gh.wait()
+    put_gwo.wait()
+    put_gwi.wait()
 
 
 def one_kernel(n, fs, hidden, w_in, decay, norm_gain, w_out, grad_out):
@@ -599,25 +619,26 @@
         V((cin, tok), bf16), V((rows_in, d), f32),
         V((outer, rows_in, d), bf16), V((outer, rows_in, d), bf16),
         V((outer, rows_in, d), bf16), V((outer, rows_in, d), bf16),
-        V((rows_in, 128), f32), V((fs, rows_in, 128), f32), V((8, d), f32), V((n, 8, d), f32),
+        V((rows_in, 128), f32), V((fs, rows_in, 128), f32), V((8, d // 8), f32), V((n, 8, d // 8), f32),
         dma((3, 2, n)), dma((2, n)), dma((3, n)), dma((3, n)), dma((5, n)), dma((5, n)),
         dma((1 + outer,)), dma((1 + outer,)), dma((2, outer)), dma((2, outer)),
         dma((2, n)), dma((2, n)), V((hp, nst), f32),
+        V((tok, d), bf16), V((tok, d), bf16), V(decay.shape, f32), V((hp,), f32),
+        V((tok, d), bf16), V((rows_in, d), f32), V((rows_out, d), f32), dma((9,)),
     ]
-    vm = pl.BlockSpec(memory_space=pltpu.VMEM)
     return pl.pallas_call(
         functools.partial(fused, n, fs, math.sqrt(tok * n), math.sqrt(d * fs)),
         out_shape=(
-            jax.ShapeDtypeStruct((tok, d), bf16),
-            jax.ShapeDtypeStruct((rows_in, d), f32),
-            jax.ShapeDtypeStruct((rows_out, d), f32),
+            V((tok, d), bf16),
+            V((rows_in, d), f32),
+            V((rows_out, d), f32),
         ),
-        in_specs=[vm] * 6,
-        out_specs=(vm, vm, vm),
+        in_specs=[pl.BlockSpec(memory_space=pl.ANY)] * 6,
+        out_specs=(pl.BlockSpec(memory_space=pl.ANY),) * 3,
         scratch_shapes=scratch,
         compiler_params=pltpu.CompilerParams(
             collective_id=0, has_side_effects=True, vmem_limit_bytes=60 * 1024 * 1024),
-    )(hidden, w_in, decay, norm_gain[:, None], w_out, grad_out)
+    )(hidden, w_in, decay, norm_gain, w_out, grad_out)
 
 
 def solution(mesh):

time: 107 us -> 94.7 us (0.89); the launches traced: 106 us -> 94.5 us
  Pallas kernels: 99.4 us -> 91.5 us
  local copies, waits for them, and re-layouts: 5.47 us -> 2.37 us
    pallas_call x1, Pallas kernels: 99.4 us -> 91.5 us  [one_kernel(): pl.pallas_call(functools.partial(fused, n, fs, math.sqrt(tok * n), math.s...]
    unnamed x9 -> x3, local copies, waits for them, and re-layouts: 4.67 us -> 2.37 us
where the time goes in v1:
time: 94.7 us; the launch traced here: 94.5 us
  Pallas kernels  91.5 us (97%)
  local copies, waits for them, and re-layouts  2.37 us (3%)
    pallas_call x1, Pallas kernels, one_kernel(): pl.pallas_call(functools.partial(fused, n, fs, math.sqrt(tok * n), math.s...  91.5 us
    unnamed x3, local copies, waits for them, and re-layouts  2.37 us

profile of v1, /device:TPU:0, one launch (start us, length us, event | category | flops | bytes accessed | tf_op | source)
XLA Modules:
  0.0 94.5 jit_solution(17050465805627049509)
XLA Ops:
  0.6 91.5 %shard_map.85 = (bf16[512,1024]{1,0:T(8,128)(2,1)S(1)}, f32[96,1024]{1,0:T(8,128)S(1)}, f32[32,1024]{1,0:T(8,128)S(1)}) custom-call(bf16[512,1024]{1,0:T(8,128)(2,1)} %hid_any.1, bf16[96,1024]{1,0:T(8,128)(2,1)} %win_ref.1, f32[4,512]{1,0:T(4,128)} %dec_any.1, f32[256]{0:T(256)} %gain_any.1, bf16[32,1024]{1,0:T(8,128)(2,1)} %wout_ref.1, ...), custom_call_target="tpu_custom_call" | custom-call | tf_op jit(solution)/shard_map/pallas_call | solution.py:629
  92.1 1.0 %copy.12 = bf16[512,1024]{1,0:T(8,128)(2,1)} copy(bf16[512,1024]{1,0:T(8,128)(2,1)S(1)} %get-tuple-element.3) | data formatting | bytes 2097152
  93.1 0.7 copy.14
  93.8 0.7 copy.13

commit v2 on v1

v2 whole, which is shorter than its diff:
```python
import functools
import math

import jax
import jax.numpy as jnp
from jax import lax
from jax.experimental import pallas as pl
from jax.experimental.pallas import tpu as pltpu
from jax.sharding import PartitionSpec as P

D = 4096
H = 4
P_SIZE = 64
N = 128
HP = 256


highest = lax.Precision.HIGHEST
clip_output = 10.0


def prefix(x, axis, combine, identity):
    count, index = (lax.axis_size(axis), lax.axis_index(axis))
    everything = jax.tree.map(lambda part: lax.all_gather(part, axis), x)
    start = jax.tree.map(
        lambda part, zero: jnp.broadcast_to(jnp.asarray(zero, part.dtype), part.shape), x, identity
    )

    def step(k, before):
        reached = k < index
        new = combine(before, jax.tree.map(lambda part: part[k], everything))
        return jax.tree.map(lambda a, b: jnp.where(reached, a, b), new, before)

    return lax.fori_loop(0, count, step, start)


def entering(x, axis, join, neutral):
    count = lax.axis_size(axis)
    place = lax.axis_index(axis)
    ahead = count - 1 - place
    gathered = jax.tree.map(
        lambda a, kind: lax.all_gather(a.astype(kind), axis),
        x,
        jax.tree.map(lambda a: jnp.bfloat16 if a.dtype == jnp.float32 else a.dtype, x),
    )
    state = jax.tree.map(lambda a, e: jnp.zeros_like(a) + jnp.asarray(e, a.dtype), x, neutral)

    def one(step, state):
        source = count - 1 - step
        return join(
            state,
            jax.tree.map(
                lambda a, own: lax.dynamic_index_in_dim(a, source, 0, False).astype(own.dtype),
                gathered,
                x,
            ),
        )

    return lax.fori_loop(0, ahead, one, state)


def split_columns(projection):
    return (
        projection[:, :HP],
        projection[:, HP : 2 * HP],
        projection[:, 2 * HP : 2 * HP + N],
        projection[:, 2 * HP + N :],
    )


def intra_block(x_part, b_part, c_part, log_decay):
    length = x_part.shape[0]
    cum_decay = jnp.cumsum(log_decay, axis=1)
    x_heads = x_part.reshape(length, H, P_SIZE)
    causal = jnp.arange(length)[:, None] >= jnp.arange(length)[None, :]
    gaps = jnp.where(causal[None], cum_decay[:, :, None] - cum_decay[:, None, :], 0.0)
    weights = jnp.where(causal[None], jnp.exp(gaps), 0.0)
    scores = jnp.dot(c_part, b_part.T, precision=highest)
    mixed = weights * scores[None]
    y_intra = jnp.einsum("hts,shp->thp", mixed, x_heads, precision=highest).reshape(
        length, H * P_SIZE
    )
    tail = jnp.exp(cum_decay[:, -1:] - cum_decay)
    weighted = x_heads * tail.T[:, :, None]
    state_part = jnp.einsum("shp,sn->hpn", weighted, b_part, precision=highest)
    return (y_intra, state_part, cum_decay)


def finish_block(gate_part, y_intra, c_part, start_state, cum_decay, norm_gain):
    length = c_part.shape[0]
    carried = jnp.einsum("hpn,tn->thp", start_state, c_part, precision=highest)
    carried = carried * jnp.exp(cum_decay).T[:, :, None]
    y_full = y_intra + carried.reshape(length, H * P_SIZE)
    gated = y_full * jax.nn.silu(gate_part)
    factor = lax.rsqrt(jnp.mean(gated * gated, axis=-1, keepdims=True) + 1e-05)
    return gated * factor * norm_gain


def carry_states(earlier, later):
    return (earlier[0] * later[0], later[0] * earlier[1] + later[1])


def carry_adjoint(earlier, later):
    return (earlier[0] * later[0], later[1] + later[0] * earlier[1])


def local(hidden, w_in, decay, norm_gain, w_out, grad_out):
    clip_input = math.sqrt(D)
    tok_rows = hidden.shape[0]
    root_tokens = math.sqrt(tok_rows * lax.axis_size("ctx"))
    contract_last = (((1,), (1,)), ((), ()))
    contract_first = (((0,), (0,)), ((), ()))
    partial_proj = lax.dot_general(
        hidden,
        lax.all_gather(w_in, "ctx", axis=0, tiled=True),
        contract_last,
        preferred_element_type=jnp.float32,
    )
    slab_out = lax.all_gather(w_out, "ctx", axis=0, tiled=True)
    partial_grad = lax.dot_general(
        grad_out, slab_out, contract_last, preferred_element_type=jnp.float32
    )
    projection, grad_normed = lax.psum((partial_proj, partial_grad), "fsdp")
    log_decay = jnp.log(decay)
    gate_part, x_part, b_part, c_part = split_columns(projection)

    def intra_only(x_value, b_value, c_value):
        return intra_block(x_value, b_value, c_value, log_decay)

    (y_intra, state_part, cum_decay), intra_pull = jax.vjp(intra_only, x_part, b_part, c_part)
    decay_total = jnp.exp(cum_decay[:, -1])[:, None, None]
    identity = (jnp.ones_like(decay_total), jnp.zeros_like(state_part))
    _, start_state = prefix((decay_total, state_part), "ctx", carry_states, identity)

    def finish_only(gate_value, intra_value, c_value, state_value):
        return finish_block(gate_value, intra_value, c_value, state_value, cum_decay, norm_gain)

    normed, finish_pull = jax.vjp(finish_only, gate_part, y_intra, c_part, start_state)
    grad_gate, grad_intra, grad_c_late, grad_start = finish_pull(grad_normed)
    _, grad_end = entering((decay_total, grad_start), "ctx", carry_adjoint, identity)
    grad_x, grad_b, grad_c_early = intra_pull((grad_intra, grad_end, jnp.zeros_like(cum_decay)))
    grad_projection = jnp.concatenate(
        [grad_gate, grad_x, grad_b, grad_c_early + grad_c_late], axis=1
    ).astype(jnp.bfloat16)
    columns = grad_projection
    grad_hidden = jnp.dot(
        columns, lax.all_gather(w_in, "ctx", axis=0, tiled=True), preferred_element_type=jnp.float32
    )
    columns = grad_projection
    raw_in = (
        lax.psum_scatter(
            lax.dot_general(columns, hidden, contract_first, preferred_element_type=jnp.float32),
            "ctx",
            scatter_dimension=0,
            tiled=True,
        )
        / root_tokens
    )
    weight_square = jnp.sum(jnp.square(w_in.astype(jnp.float32)), axis=1)
    weight_in, grad_in = lax.psum((weight_square, jnp.sum(raw_in * raw_in, axis=1)), "fsdp")
    factor_in = jnp.minimum(
        1.0,
        clip_input
        * jnp.maximum(jnp.sqrt(weight_in), 0.001)
        / jnp.maximum(jnp.sqrt(grad_in), 1e-06),
    )
    normed_rounded = normed.astype(jnp.bfloat16)
    weight_out = jnp.sqrt(jnp.sum(jnp.square(slab_out.astype(jnp.float32)), axis=0))
    raw_out = (
        lax.psum_scatter(
            lax.dot_general(
                normed_rounded, grad_out, contract_first, preferred_element_type=jnp.float32
            ),
            "ctx",
            scatter_dimension=0,
            tiled=True,
        )
        / root_tokens
    )
    grad_square = lax.psum(jnp.sum(raw_out * raw_out, axis=0), "ctx")
    factor_out = jnp.minimum(
        1.0,
        clip_output * jnp.maximum(weight_out, 0.001) / jnp.maximum(jnp.sqrt(grad_square), 1e-06),
    )
    return (
        grad_hidden.astype(jnp.bfloat16),
        raw_in * factor_in[:, None],
        raw_out * factor_out[None, :],
    )


NN = (((1,), (0,)), ((), ()))
NT = (((1,), (1,)), ((), ()))
TN = (((0,), (0,)), ((), ()))
MESH = pl.DeviceIdType.MESH
f32 = jnp.float32
bf16 = jnp.bfloat16
EPS = 1e-05


def split(a):
    hi = a.astype(bf16)
    return hi, (a - hi.astype(f32)).astype(bf16)


def dot1(a, b, dims):
    return lax.dot_general(a, b, dims, preferred_element_type=f32)


def dot3(a, b, dims):
    return dot1(a[0], b[0], dims) + (dot1(a[0], b[1], dims) + dot1(a[1], b[0], dims))


def transposed(pair):
    return pair[0].T, pair[1].T


def early_and_late(n, rows, hp, nst):
    g = math.gcd(rows, math.gcd(hp, nst))
    early, late = [], []
    for y in (0, 1):
        first, last = [], []
        for q in range(n // 2):
            for j in range(rows // g):
                row = (q * 2 + y) * rows + j * g
                soon = row + g <= hp or row >= 2 * hp + nst
                (first if soon else last).append((row, q, j))
        early.append(first)
        late.append(last)
    return g, early, late


def fits(n, w_in, w_out):
    rows, hp = w_in.shape[0], w_out.shape[0] * n
    nst = (rows * n - 2 * hp) // 2
    g, early, late = early_and_late(n, rows, hp, nst)
    same = len(early[0]) == len(early[1]) and len(early[0]) >= 2
    return g % 16 == 0 and same and w_in.shape[1] % 1024 == 0


def fused(
    n, fs, root_tokens, clip_input,
    hid_any, win_ref, dec_any, gain_any, wout_ref, gout_any,
    gh_any, gwi_any, gwo_any,
    hidT, goutT, wi_all, wo_all, pT,
    bi, ai_in, xi_out, xi_in, ci_in, bo, ao_in, xo_out, xo_in, co_in,
    e_out, e_all, e_ref, st_out, st_all, s0_ref, ad_out, ad_all, g_ref,
    ro, ob1, ob1r, ob2, ob2r, gp, rin, ri, ib1, ib1r, ib2, ib2r,
    nin_out, nin_all, nout_out, nout_all,
    g_send, g_recv, pi_send, pi_recv, po_send, po_recv, s_send, s_recv, t_send, t_recv,
    o_send, o_recv, i_send, iy_recv, iz_recv, n_send, n_recv, tmp,
    hid_ref, gout_ref, dec_ref, gain_ref, gh_ref, gwi_ref, gwo_ref, l_sem,
):
    c = lax.axis_index("ctx")
    f = lax.axis_index("fsdp")
    outer = n // 2
    z, y = c // 2, lax.rem(c, 2)
    yn = c + 1 - 2 * y
    core = lax.rem(f, 2)
    fcore = f + 1 - 2 * core
    fx = lax.rem(f + fs // 2, fs)
    rows_in, d = win_ref.shape
    rows_out = wout_ref.shape[0]
    tok = hid_any.shape[0]
    cin, hp = rows_in * n, rows_out * n
    nst = (cin - 2 * hp) // 2
    hpf = hp // fs
    first = hp // rows_in
    g, early, late = early_and_late(n, rows_in, hp, nst)

    def copy(src, dst, ssem, rsem, dev):
        return pltpu.make_async_remote_copy(
            src_ref=src, dst_ref=dst, send_sem=ssem, recv_sem=rsem,
            device_id=dev, device_id_type=MESH)

    ends = []

    def under(has, fn, *args):
        if has is None:
            fn(*args)
        else:
            pl.when(has)(lambda: fn(*args))

    def start(*args, when=None):
        under(when, lambda: copy(*args).start())

    def go(*args, when=None):
        start(*args, when=when)
        ends.append((when, args))

    def total(src, dst, sem, rsem, when=None):
        ends.append((when, (src, dst, sem, rsem, (yn, f))))

    local = [
        pltpu.make_async_copy(src, dst, l_sem.at[i])
        for i, (src, dst) in enumerate((
            (hid_any, hid_ref), (win_ref, wi_all.at[c]), (gout_any, gout_ref),
            (wout_ref, wo_all.at[c]), (dec_any, dec_ref), (gain_any, gain_ref)))
    ]
    for each in local:
        each.start()

    barrier = pltpu.get_barrier_semaphore()
    for k in range(1, n):
        pl.semaphore_signal(barrier, inc=1, device_id=(lax.rem(c + k, n), f), device_id_type=MESH)
    for k in range(1, fs):
        pl.semaphore_signal(barrier, inc=1, device_id=(c, lax.rem(f + k, fs)), device_id_type=MESH)
    pl.semaphore_wait(barrier, n + fs - 2)

    both = ((win_ref, wi_all), (wout_ref, wo_all))
    up = jnp.minimum(z + 1, outer - 1) * 2 + y
    down = jnp.maximum(z - 1, 0) * 2 + y

    pieces = (rows_in // g, 1)

    def part(ref, a, s, j):
        return ref.at[s] if a else ref.at[s, pl.ds(j * g, g)]

    def own(a):
        src, dst = both[a]
        for j in range(pieces[a]):
            to = part(dst, a, c, j)
            at = src if a else src.at[pl.ds(j * g, g)]
            sem = g_recv.at[a, c, j]
            start(at, to, g_send.at[0, a], sem, (up, f), when=z < outer - 1)
            start(at, to, g_send.at[1, a], sem, (down, f), when=z > 0)
            start(at, to, g_send.at[2, a], sem, (yn, f))

    def landed_part(a, s, j):
        at = part(both[a][1], a, s, j)
        copy(at, at, g_send.at[2, a], g_recv.at[a, s, j], (yn, f)).wait_recv()

    def landed(a, s):
        for j in range(pieces[a]):
            landed_part(a, s, j)

    def relay(a, s, fwd, j):
        at = part(both[a][1], a, s, j)
        has, to, way = fwd
        landed_part(a, s, j)
        start(at, at, g_send.at[way, a], g_recv.at[a, s, j], (to, f), when=has)
        start(at, at, g_send.at[2, a], g_recv.at[a, s, j], (yn, f))

    own(0)
    for each in local[:2]:
        each.wait()
    hidT[...] = hid_ref[...].T

    hi = rows_in // 2
    mine = pl.ds(pl.multiple_of(core * hi, 8), hi)
    other = pl.ds(pl.multiple_of((1 - core) * hi, 8), hi)
    mine_o = pl.ds(pl.multiple_of(core * rows_out, 8), rows_out)
    other_o = pl.ds(pl.multiple_of((1 - core) * rows_out, 8), rows_out)

    class Chain:
        def __init__(self, part, pair_in, x_out, x_in, back_in, send, recv, mine, other, base):
            self.part, self.pair_in, self.x_out, self.x_in = part, pair_in, x_out, x_in
            self.back_in, self.send, self.recv, self.base = back_in, send, recv, base
            self.mine, self.other, self.half = mine, other, pair_in.shape[1]

        def to_pair(self, s):
            return copy(self.part.at[s, self.other], self.pair_in.at[s], self.send.at[0],
                        self.recv.at[0, s], (c, fcore))

        def across(self, s):
            return copy(self.x_out.at[s], self.x_in.at[s], self.send.at[1],
                        self.recv.at[1, s], (c, fx))

        def back(self, s):
            return copy(self.part.at[s, self.mine], self.back_in.at[s], self.send.at[2],
                        self.recv.at[2, s], (c, fcore))

        def place(self, s, which, value):
            at = self.base + s * (2 * self.half) + which * self.half
            pT[pl.ds(pl.multiple_of(at, 8), self.half), :] = value

        def take(self, s, value):
            self.part[s] = value
            self.to_pair(s).start()

        def pair_sum(self, s):
            self.to_pair(s).wait_recv()
            value = self.part[s, self.mine] + self.pair_in[s]
            self.part[s, self.mine] = value
            self.x_out[s] = value.astype(bf16)
            self.across(s).start()

        def full_sum(self, s):
            self.across(s).wait_recv()
            value = self.part[s, self.mine] + self.x_in[s].astype(f32)
            self.part[s, self.mine] = value
            self.back(s).start()
            self.place(s, core, value)

        def collect(self, s):
            self.back(s).wait_recv()
            self.place(s, 1 - core, self.back_in[s])

        def finish(self):
            total(self.pair_in, self.pair_in, self.send.at[0], self.recv.at[0, 0])
            total(self.x_out, self.x_in, self.send.at[1], self.recv.at[1, 0])
            total(self.back_in, self.back_in, self.send.at[2], self.recv.at[2, 0])

    ins = Chain(bi, ai_in, xi_out, xi_in, ci_in, pi_send, pi_recv, mine, other, 0)
    outs = Chain(bo, ao_in, xo_out, xo_in, co_in, po_send, po_recv, mine_o, other_o, cin)

    def both_true(a, b):
        return b if a is None else jnp.logical_and(a, b)

    def row(k, way):
        there = z - k if way == 0 else z + k
        has = there >= 0 if way == 0 else there < outer
        q = jnp.maximum(there, 0) if way == 0 else jnp.minimum(there, outer - 1)
        fwd = (z < outer - 1, up, 0) if way == 0 else (z > 0, down, 1)
        return has, q, fwd

    def take_in(s):
        ins.take(s, dot1(wi_all[s], hidT[...], NN))

    def soon(has, s):
        return both_true(has, s >= first)

    def behind(k):
        if k == 0:
            own(1)
            return
        for j in range(pieces[0]):
            for way in (0, 1):
                has, q, fwd = row(k, way)
                s = q * 2 + y
                under(both_true(has, s < first), relay, 0, s, fwd, j)
        for way in (0, 1):
            has, q, fwd = row(k, way)
            under(has, relay, 1, q * 2 + y, fwd, 0)

    def ahead(k):
        for j in range(pieces[0]):
            for way in (0, 1):
                has, q, fwd = row(k, way)
                s = q * 2 + y
                under(soon(has, s), relay, 0, s, fwd, j)

    def crossed(s):
        landed(0, s)
        take_in(s)

    def run(steps, lags):
        done = []

        def trail(i):
            for lag, name in zip(lags, ("pair_sum", "full_sum", "collect")):
                if 0 <= i - lag < len(done):
                    has, s, chain = done[i - lag]
                    under(has, getattr(chain, name), s)

        for has, fn, arg, chain in steps:
            under(has, fn, arg)
            if chain is not None:
                done.append((has, arg, chain))
                trail(len(done) - 1)

        def rest():
            for i in range(len(done), len(done) + lags[-1]):
                trail(i)

        return rest

    steps = [(soon(None, c), take_in, c, ins), (None, ahead, 1, None)]
    later = [(soon(None, yn), crossed, yn, ins)]
    for k in range(1, outer):
        if k > 1:
            steps.append((None, ahead, k, None))
        for way in (0, 1):
            has, q, _ = row(k, way)
            s = q * 2 + y
            steps.append((soon(has, s), take_in, s, ins))
        steps.extend(later)
        steps.append((None, behind, k - 1, None))
        later = []
        for way in (0, 1):
            has, q, _ = row(k, way)
            s = q * 2 + 1 - y
            later.append((soon(has, s), crossed, s, ins))
    steps.extend(later)

    def decays():
        decay = dec_ref[...]
        lane = lax.broadcasted_iota(jnp.int32, decay.shape, 1)
        shift = 1
        while shift < tok:
            decay = decay * jnp.where(lane >= shift, pltpu.roll(decay, shift, 1), 1.0)
            shift *= 2
        heads = decay.shape[0]
        for h in range(heads):
            e_ref[h * (hp // heads) : (h + 1) * (hp // heads), :] = jnp.broadcast_to(
                decay[h : h + 1], (hp // heads, tok))
        e_out[...] = jnp.broadcast_to(
            e_ref[pl.ds(pl.multiple_of(f * hpf, 8), 8), tok - 128 : tok][:, 127:128], (8, nst))
        e_all[c] = e_out[...]
        for k in range(1, n):
            start(e_out, e_all.at[c], t_send.at[0], t_recv.at[0, c], (lax.rem(c + k, n), f))
        total(e_all.at[pl.ds(0, n - 1)], e_all.at[pl.ds(0, n - 1)], t_send.at[0], t_recv.at[0, 0])

    for each in local[2:]:
        each.wait()
    goutT[...] = gout_ref[...].T
    decays()
    run(steps, (2, 5, 8))()

    e = e_ref[...]
    einv = 1.0 / e
    eend = e[:, tok - 1 : tok]
    xs = pT[hp : 2 * hp, :] * einv
    bT = pT[2 * hp : 2 * hp + nst, :]
    cT = pT[2 * hp + nst : cin, :]
    xs2, b2, c2 = split(xs), split(bT), split(cT)
    tmp[...] = dot3(xs2, b2, NT) * eend
    own_rows = pl.ds(pl.multiple_of(f * hpf, 8), hpf)
    st_out[...] = tmp[own_rows, :]
    for k in range(n - 1, 0, -1):
        go(st_out, st_all.at[c], s_send.at[0, k], s_recv.at[0, c],
           (jnp.minimum(c + k, n - 1), f), when=c + k < n)

    upper = lax.broadcasted_iota(jnp.int32, (tok, tok), 0) <= lax.broadcasted_iota(
        jnp.int32, (tok, tok), 1)
    scores2 = split(jnp.where(upper, dot3(transposed(b2), c2, NN), 0.0))
    y_in = dot3(xs2, scores2, NN)
    behind(outer - 1)

    def take_gate(s):
        under(lax.rem(s + y, 2) != 0, landed, 0, s)
        take_in(s)

    def take_out(q):
        landed(1, q * 2 + 1 - y)
        at = pl.ds(pl.multiple_of(q * 2, 2), 2)
        outs.take(q, dot1(wo_all[at].reshape(2 * rows_out, d), goutT[...], NN))

    more = [(None, take_out, z, outs)]
    for k in range(1, outer):
        if k == outer - 1:
            more.extend((None, take_gate, s, ins) for s in range(first))
        for way in (0, 1):
            has, q, _ = row(k, way)
            more.append((has, take_out, q, outs))
    rest = run(more, (2, 4, 6))

    for k in range(1, n):
        s = lax.rem(c + n - k, n)
        copy(e_out, e_all.at[s], t_send.at[0], t_recv.at[0, s], (s, f)).wait_recv()
        s = jnp.maximum(c - k, 0)
        pl.when(c - k >= 0)(lambda s=s, k=k: copy(
            st_out, st_all.at[s], s_send.at[0, k], s_recv.at[0, s], (s, f)).wait_recv())
    state = jnp.zeros((hpf, nst), f32)
    for k in range(n - 1):
        new = e_all[k, 0:1, :] * state + st_all[k]
        state = jnp.where(k < c, new, state)
    s0_ref[own_rows, :] = state

    def share(ref, i):
        for k in range(1, fs):
            start(ref.at[own_rows], ref.at[own_rows], t_send.at[i], t_recv.at[i, f],
                  (c, lax.rem(f + k, fs)))
        total(st_all.at[pl.ds(0, fs - 1)], st_all.at[pl.ds(0, fs - 1)], t_send.at[i],
              t_recv.at[i, 0])

    def shared(ref, i):
        for k in range(1, fs):
            p = lax.rem(f + fs - k, fs)
            rows = pl.ds(pl.multiple_of(p * hpf, 8), hpf)
            copy(ref.at[rows], ref.at[rows], t_send.at[i], t_recv.at[i, p], (c, p)).wait_recv()

    share(s0_ref, 1)
    rest()
    gate = pT[:hp, :]
    sig = 1.0 / (1.0 + jnp.exp(-gate))
    silu = gate * sig

    shared(s0_ref, 1)
    s02 = split(s0_ref[...])
    yT = (y_in + dot3(s02, c2, NN)) * e

    gain = jnp.broadcast_to(gain_ref[...].reshape(1, hp), (8, hp)).T[:, 0:1]
    gated = yT * silu
    r = lax.rsqrt(jnp.mean(gated * gated, axis=0, keepdims=True) + EPS)
    normed = (gated * r * gain).astype(bf16)
    u = pT[cin:, :] * gain
    dgated = r * u - gated * (r * r * r * jnp.mean(u * gated, axis=0, keepdims=True))
    dys2 = split(dgated * silu * e)
    tmp[...] = dot3(dys2, c2, NT)
    ad_out[...] = tmp[own_rows, :].astype(bf16)
    for k in range(n - 1, 0, -1):
        go(ad_out, ad_all.at[c], s_send.at[1, k], s_recv.at[1, c],
           (jnp.maximum(c - k, 0), f), when=c - k >= 0)

    ro[...] = dot1(normed, gout_ref[...], NN)
    for q in range(outer):
        at = pl.ds(pl.multiple_of((q * 2 + 1 - y) * rows_out, 8), rows_out)
        ob1[q] = ro[at, :].astype(bf16)
    go(ob1, ob1r, o_send.at[0], o_recv.at[0], (yn, f))

    blocks = [early[0] + late[0], early[1] + late[1]]
    n_early, n_blocks = len(early[0]), len(blocks[0])

    def pick(i, part, side):
        a, b = blocks[0][i][part], blocks[1][i][part]
        return a + side * (b - a)

    def to_partner(lo, hi):
        for i in range(lo, hi):
            at = pl.ds(pl.multiple_of(pick(i, 0, 1 - y), 8), g)
            ib1[i] = rin[at, :].astype(bf16)
            start(ib1.at[i], ib1r.at[i], i_send.at[0], iy_recv.at[i], (yn, f))

    def merge(lo, hi):
        for i in range(lo, hi):
            copy(ib1.at[i], ib1r.at[i], i_send.at[0], iy_recv.at[i], (yn, f)).wait_recv()
            at = pl.ds(pl.multiple_of(pick(i, 0, y), 8), g)
            value = rin[at, :] + ib1r[i].astype(f32)
            q, j = pick(i, 1, y), pick(i, 2, y)

            def keep():
                ri[pl.ds(pl.multiple_of(j * g, 8), g), :] = value

            def send():
                ib2[i] = value.astype(bf16)
                copy(ib2.at[i], ib2r.at[z, j], i_send.at[1], iz_recv.at[0], (q * 2 + y, f)).start()

            pl.when(q == z)(keep)
            pl.when(q != z)(send)

    dscores = jnp.where(upper, dot1(xs2[0].T, dys2[0], NN), 0.0).astype(bf16)
    gp[:hp, :] = (dgated * yT * (sig * (1.0 + gate * (1.0 - sig)))).astype(bf16)
    rin[:hp, :] = dot1(gp[:hp, :], hid_ref[...], NN)
    gp[2 * hp + nst :, :] = (dot1(b2[0], dscores, NN) + dot3(transposed(s02), dys2, NN)).astype(bf16)
    rin[2 * hp + nst :, :] = dot1(gp[2 * hp + nst :, :], hid_ref[...], NN)
    to_partner(0, n_early)
    db = dot1(c2[0], dscores, NT)
    dxs = dot1(dys2[0], scores2[0], NT)

    for k in range(1, n):
        s = jnp.minimum(c + k, n - 1)
        pl.when(c + k < n)(lambda s=s, k=k: copy(
            ad_out, ad_all.at[s], s_send.at[1, k], s_recv.at[1, s], (s, f)).wait_recv())
    adj = jnp.zeros((hpf, nst), f32)
    for k in range(n - 1, 0, -1):
        new = e_all[k, 0:1, :] * adj + ad_all[k].astype(f32)
        adj = jnp.where(k > c, new, adj)
    g_ref[own_rows, :] = adj
    share(g_ref, 2)

    copy(ob1, ob1r, o_send.at[0], o_recv.at[0], (yn, f)).wait_recv()
    for q in range(outer):
        at = pl.ds(pl.multiple_of((q * 2 + y) * rows_out, 8), rows_out)
        value = ro[at, :] + ob1r[q].astype(f32)
        ro[at, :] = value
        ob2[q] = value.astype(bf16)
    for k in range(1, outer):
        q = lax.rem(z + k, outer)
        start(ob2.at[q], ob2r.at[z], o_send.at[1], o_recv.at[1], (q * 2 + y, f))
    some = pl.ds(0, outer - 1)
    total(ob2.at[some], ob2r.at[some], o_send.at[1], o_recv.at[1])

    merge(0, 2)
    shared(g_ref, 2)
    g2 = split(g_ref[...] * eend)
    gp[hp : 2 * hp, :] = ((dxs + dot3(g2, b2, NN)) * einv).astype(bf16)
    gp[2 * hp : 2 * hp + nst, :] = (db + dot3(transposed(g2), xs2, NN)).astype(bf16)
    rin[hp : 2 * hp + nst, :] = dot1(gp[hp : 2 * hp + nst, :], hid_ref[...], NN)
    to_partner(n_early, n_blocks)
    total(ib1, ib1r, i_send.at[0], iy_recv.at[0])
    merge(2, n_early)

    gpt = gp[...].T
    wi = wi_all[...].reshape(cin, d)
    gh_ref[...] = dot1(gpt, wi, NN).astype(bf16)
    put_gh = pltpu.make_async_copy(gh_ref, gh_any, l_sem.at[6])
    put_gh.start()

    weight = jnp.zeros((1, d), f32)
    for s in range(n):
        w = wo_all[s].astype(f32)
        weight = weight + jnp.sum(w * w, axis=0, keepdims=True)
    w = wi_all[c].astype(f32)
    weight_in = jnp.sum(w * w, axis=1, keepdims=True)

    copy(ob2.at[some], ob2r.at[some], o_send.at[1], o_recv.at[1], (yn, f)).wait_recv()
    acc = ro[pl.ds(pl.multiple_of(c * rows_out, 8), rows_out), :]
    for k in range(1, outer):
        q = lax.rem(z + k, outer)
        acc = acc + ob2r[q].astype(f32)
    acc = acc * (1.0 / root_tokens)
    ro[:rows_out, :] = acc
    nout_out[...] = jnp.sum(acc * acc, axis=0, keepdims=True).reshape(8, d // 8)
    for k in range(1, n):
        start(nout_out, nout_all.at[c], n_send.at[0], n_recv.at[0, c], (lax.rem(c + k, n), f))
    total(nout_all.at[pl.ds(0, n - 1)], nout_all.at[pl.ds(0, n - 1)], n_send.at[0], n_recv.at[0, 0])
    nout_all[c] = nout_out[...]

    merge(n_early, n_blocks)
    sent = n_blocks - rows_in // g
    most = pl.ds(0, sent)
    total(ib2.at[most], ib2.at[most], i_send.at[1], iz_recv.at[0])

    copy(ib2r.at[some], ib2r.at[some], i_send.at[1], iz_recv.at[0], (yn, f)).wait_recv()
    acc = ri[...]
    for k in range(1, outer):
        q = lax.rem(z + k, outer)
        acc = acc + ib2r[q].reshape(rows_in, d).astype(f32)
    acc = acc * (1.0 / root_tokens)
    ri[...] = acc
    at = lax.broadcasted_iota(jnp.int32, (rows_in, 128), 1)
    sums = jnp.where(at < 8, jnp.sum(acc * acc, axis=1, keepdims=True), weight_in)
    nin_out[...] = sums.T[:16, :]
    for k in range(1, fs):
        start(nin_out, nin_all.at[f], n_send.at[1], n_recv.at[1, f], (c, lax.rem(f + k, fs)))
    total(nin_all.at[pl.ds(0, fs - 1)], nin_all.at[pl.ds(0, fs - 1)], n_send.at[1], n_recv.at[1, 0])
    nin_all[f] = nin_out[...]

    grad_square = nout_all[c]
    for k in range(1, n):
        s = lax.rem(c + n - k, n)
        copy(nout_out, nout_all.at[s], n_send.at[0], n_recv.at[0, s], (s, f)).wait_recv()
        grad_square = grad_square + nout_all[s]
    grad_square = grad_square.reshape(1, d)
    factor = jnp.minimum(1.0, clip_output * jnp.maximum(jnp.sqrt(weight), 0.001)
                         / jnp.maximum(jnp.sqrt(grad_square), 1e-06))
    gwo_ref[...] = ro[:rows_out, :] * factor
    put_gwo = pltpu.make_async_copy(gwo_ref, gwo_any, l_sem.at[7])
    put_gwo.start()

    square = nin_all[f]
    for k in range(1, fs):
        p = lax.rem(f + fs - k, fs)
        copy(nin_out, nin_all.at[p], n_send.at[1], n_recv.at[1, p], (c, p)).wait_recv()
        square = square + nin_all[p]
    root = jnp.sqrt(square)
    factor = jnp.minimum(1.0, clip_input * jnp.maximum(root[8:16], 0.001)
                         / jnp.maximum(root[0:8], 1e-06))
    gwi_ref[...] = ri[...] * factor.T[:, 0:1]
    put_gwi = pltpu.make_async_copy(gwi_ref, gwi_any, l_sem.at[8])
    put_gwi.start()

    ins.finish()
    outs.finish()
    for a, (_, ref) in enumerate(both):
        for at in range(outer):
            if at < outer - 1:
                part = ref.at[pl.ds(0, at + 1)]
                total(part, part, g_send.at[0, a], g_recv.at[a, 0], z == at)
            if at > 0:
                part = ref.at[pl.ds(0, outer - at)]
                total(part, part, g_send.at[1, a], g_recv.at[a, 0], z == at)
        part = ref.at[pl.ds(0, outer)]
        total(part, part, g_send.at[2, a], g_recv.at[a, 0])
    for has, args in ends:
        under(has, lambda args=args: copy(*args).wait_send())
    put_gh.wait()
    put_gwo.wait()
    put_gwi.wait()


def one_kernel(n, fs, hidden, w_in, decay, norm_gain, w_out, grad_out):
    tok, d = hidden.shape
    rows_in, rows_out = w_in.shape[0], w_out.shape[0]
    cin, hp = rows_in * n, rows_out * n
    nst = (cin - 2 * hp) // 2
    hpf, outer = hp // fs, n // 2
    hi = rows_in // 2
    g, early, late = early_and_late(n, rows_in, hp, nst)
    per, blocks = rows_in // g, len(early[0]) + len(late[0])
    V = pltpu.VMEM
    dma = pltpu.SemaphoreType.DMA
    scratch = [
        V((d, tok), bf16), V((d, tok), bf16), V((n, rows_in, d), bf16), V((n, rows_out, d), bf16),
        V((cin + hp, tok), f32),
        V((n, rows_in, tok), f32), V((n, hi, tok), f32), V((n, hi, tok), bf16),
        V((n, hi, tok), bf16), V((n, hi, tok), f32),
        V((outer, 2 * rows_out, tok), f32), V((outer, rows_out, tok), f32),
        V((outer, rows_out, tok), bf16), V((outer, rows_out, tok), bf16),
        V((outer, rows_out, tok), f32),
        V((8, nst), f32), V((n, 8, nst), f32),
        V((hp, tok), f32), V((hpf, nst), f32), V((n, hpf, nst), f32), V((hp, nst), f32),
        V((hpf, nst), bf16), V((n, hpf, nst), bf16), V((hp, nst), f32),
        V((hp, d), f32), V((outer, rows_out, d), bf16), V((outer, rows_out, d), bf16),
        V((outer, rows_out, d), bf16), V((outer, rows_out, d), bf16),
        V((cin, tok), bf16), V((cin, d), f32), V((rows_in, d), f32),
        V((blocks, g, d), bf16), V((blocks, g, d), bf16),
        V((blocks, g, d), bf16), V((outer, per, g, d), bf16),
        V((16, rows_in), f32), V((fs, 16, rows_in), f32),
        V((8, d // 8), f32), V((n, 8, d // 8), f32),
        dma((3, 2)), dma((2, n, per)), dma((3,)), dma((3, n)), dma((3,)), dma((3, outer)),
        dma((2, n)), dma((2, n)), dma((3,)), dma((3, n)),
        dma((2,)), dma((2,)), dma((2,)), dma((blocks,)), dma((1,)),
        dma((2,)), dma((2, n)), V((hp, nst), f32),
        V((tok, d), bf16), V((tok, d), bf16), V(decay.shape, f32), V((hp,), f32),
        V((tok, d), bf16), V((rows_in, d), f32), V((rows_out, d), f32), dma((9,)),
    ]
    return pl.pallas_call(
        functools.partial(fused, n, fs, math.sqrt(tok * n), math.sqrt(d * fs)),
        out_shape=(
            V((tok, d), bf16),
            V((rows_in, d), f32),
            V((rows_out, d), f32),
        ),
        in_specs=[pl.BlockSpec(memory_space=pl.ANY)] * 6,
        out_specs=(pl.BlockSpec(memory_space=pl.ANY),) * 3,
        scratch_shapes=scratch,
        compiler_params=pltpu.CompilerParams(
            collective_id=0, has_side_effects=True, vmem_limit_bytes=60 * 1024 * 1024),
    )(hidden, w_in, decay, norm_gain, w_out, grad_out)


def solution(mesh):
    n, fs = mesh.shape["ctx"], mesh.shape["fsdp"]

    def body(hidden, w_in, decay, norm_gain, w_out, grad_out):
        whole_tiles = w_in.shape[0] % 32 == 0 and w_out.shape[0] % 16 == 0 and n % 2 == 0
        if whole_tiles and fs == decay.shape[0] and fs % 2 == 0 and n >= 4 and fits(n, w_in, w_out):
            return one_kernel(n, fs, hidden, w_in, decay, norm_gain, w_out, grad_out)
        return local(hidden, w_in, decay, norm_gain, w_out, grad_out)

    return jax.shard_map(
        body,
        mesh=mesh,
        in_specs=(
            P("ctx", "fsdp"),
            P("ctx", "fsdp"),
            P(None, "ctx"),
            P(),
            P("ctx", "fsdp"),
            P("ctx", "fsdp"),
        ),
        out_specs=(P("ctx", "fsdp"), P("ctx", "fsdp"), P("ctx", "fsdp")),
        check_vma=False,
    )
```

time: 94.7 us -> 90.1 us (0.951)
  the two profiles are of different devices: /device:TPU:0 before, /device:TPU:25 now
where the time goes in v2:
time: 90.1 us; the launch traced here: 89.9 us
  Pallas kernels  86.9 us (96%)
  local copies, waits for them, and re-layouts  2.37 us (3%)
    pallas_call x1, Pallas kernels, one_kernel(): pl.pallas_call(functools.partial(fused, n, fs, math.sqrt(tok * n), math.s...  86.9 us
    unnamed x3, local copies, waits for them, and re-layouts  2.37 us

profile of v2, /device:TPU:25, one launch (start us, length us, event | category | flops | bytes accessed | tf_op | source)
XLA Modules:
  0.0 89.9 jit_solution(8190749096411027942)
XLA Ops:
  0.6 86.9 %shard_map.85 = (bf16[512,1024]{1,0:T(8,128)(2,1)S(1)}, f32[96,1024]{1,0:T(8,128)S(1)}, f32[32,1024]{1,0:T(8,128)S(1)}) custom-call(bf16[512,1024]{1,0:T(8,128)(2,1)} %hid_any.1, bf16[96,1024]{1,0:T(8,128)(2,1)} %win_ref.1, f32[4,512]{1,0:T(4,128)} %dec_any.1, f32[256]{0:T(256)} %gain_any.1, bf16[32,1024]{1,0:T(8,128)(2,1)} %wout_ref.1, ...), custom_call_target="tpu_custom_call" | custom-call | tf_op jit(solution)/shard_map/pallas_call | solution.py:799
  87.6 1.0 %copy.12 = bf16[512,1024]{1,0:T(8,128)(2,1)} copy(bf16[512,1024]{1,0:T(8,128)(2,1)S(1)} %get-tuple-element.3) | data formatting | bytes 2097152
  88.5 0.7 copy.14
  89.2 0.7 copy.13

commit v3 on v2

--- a/solution.py
+++ b/solution.py
@@ -235,7 +235,7 @@
     nst = (rows * n - 2 * hp) // 2
     g, early, late = early_and_late(n, rows, hp, nst)
     same = len(early[0]) == len(early[1]) and len(early[0]) >= 2
-    return g % 16 == 0 and same and w_in.shape[1] % 1024 == 0
+    return g % 16 == 0 and same and n % 4 == 0 and w_in.shape[1] % 1024 == 0
 
 
 def fused(
@@ -245,15 +245,16 @@
     hidT, goutT, wi_all, wo_all, pT,
     bi, ai_in, xi_out, xi_in, ci_in, bo, ao_in, xo_out, xo_in, co_in,
     e_out, e_all, e_ref, st_out, st_all, s0_ref, ad_out, ad_all, g_ref,
-    ro, ob1, ob1r, ob2, ob2r, gp, rin, ri, ib1, ib1r, ib2, ib2r,
+    ro, ob1, ob1r, ob2, ob2r, gp, rin, ri, ib1, ib1r, ib2, ib2r, irx,
     nin_out, nin_all, nout_out, nout_all,
     g_send, g_recv, pi_send, pi_recv, po_send, po_recv, s_send, s_recv, t_send, t_recv,
-    o_send, o_recv, i_send, iy_recv, iz_recv, n_send, n_recv, tmp,
+    o_send, o_recv, i_send, iy_recv, iz_recv, ir_recv, n_send, n_recv, tmp,
     hid_ref, gout_ref, dec_ref, gain_ref, gh_ref, gwi_ref, gwo_ref, l_sem,
 ):
     c = lax.axis_index("ctx")
     f = lax.axis_index("fsdp")
     outer = n // 2
+    half = outer // 2
     z, y = c // 2, lax.rem(c, 2)
     yn = c + 1 - 2 * y
     core = lax.rem(f, 2)
@@ -266,6 +267,7 @@
     nst = (cin - 2 * hp) // 2
     hpf = hp // fs
     first = hp // rows_in
+    side = z // half
     g, early, late = early_and_late(n, rows_in, hp, nst)
 
     def copy(src, dst, ssem, rsem, dev):
@@ -301,27 +303,39 @@
         each.start()
 
     barrier = pltpu.get_barrier_semaphore()
-    for k in range(1, n):
-        pl.semaphore_signal(barrier, inc=1, device_id=(lax.rem(c + k, n), f), device_id_type=MESH)
-    for k in range(1, fs):
-        pl.semaphore_signal(barrier, inc=1, device_id=(c, lax.rem(f + k, fs)), device_id_type=MESH)
-    pl.semaphore_wait(barrier, n + fs - 2)
-
-    both = ((win_ref, wi_all), (wout_ref, wo_all))
     up = jnp.minimum(z + 1, outer - 1) * 2 + y
     down = jnp.maximum(z - 1, 0) * 2 + y
+    beside = [(z < outer - 1, (up, f)), (z > 0, (down, f))]
+    for has, to in beside + [(None, (yn, f)), (None, (c, fcore)), (None, (c, fx))]:
+        under(has, lambda to=to: pl.semaphore_signal(
+            barrier, inc=1, device_id=to, device_id_type=MESH))
+    pl.semaphore_wait(
+        barrier, 3 + jnp.minimum(z, 1) + jnp.minimum(outer - 1 - z, 1))
+
+    both = ((win_ref, wi_all), (wout_ref, wo_all))
 
     pieces = (rows_in // g, 1)
 
     def part(ref, a, s, j):
         return ref.at[s] if a else ref.at[s, pl.ds(j * g, g)]
 
-    def own(a):
-        src, dst = both[a]
-        for j in range(pieces[a]):
-            to = part(dst, a, c, j)
-            at = src if a else src.at[pl.ds(j * g, g)]
-            sem = g_recv.at[a, c, j]
+    def own_y():
+        start(wout_ref, wo_all.at[c], g_send.at[2, 1], g_recv.at[1, c, 0], (yn, f))
+
+    def own_out():
+        for src, s, way in ((wout_ref, c, 0), (wo_all.at[yn], yn, 1)):
+            if way:
+                landed(1, yn)
+            for k in range(outer - 1, 0, -1):
+                q = lax.rem(z + k, outer)
+                start(src, wo_all.at[s], g_send.at[way, 1], g_recv.at[1, s, 0], (q * 2 + y, f))
+
+    def own_in():
+        a = 0
+        for j in range(pieces[0]):
+            to = part(wi_all, 0, c, j)
+            at = win_ref.at[pl.ds(j * g, g)]
+            sem = g_recv.at[0, c, j]
             start(at, to, g_send.at[0, a], sem, (up, f), when=z < outer - 1)
             start(at, to, g_send.at[1, a], sem, (down, f), when=z > 0)
             start(at, to, g_send.at[2, a], sem, (yn, f))
@@ -334,14 +348,18 @@
         for j in range(pieces[a]):
             landed_part(a, s, j)
 
-    def relay(a, s, fwd, j):
+    def relay(s, fwd, j):
+        at = part(wi_all, 0, s, j)
+        has, to, way = fwd
+        landed_part(0, s, j)
+        start(at, at, g_send.at[way, 0], g_recv.at[0, s, j], (to, f), when=has)
+
+    def cross(a, s, j):
         at = part(both[a][1], a, s, j)
-        has, to, way = fwd
-        landed_part(a, s, j)
-        start(at, at, g_send.at[way, a], g_recv.at[a, s, j], (to, f), when=has)
         start(at, at, g_send.at[2, a], g_recv.at[a, s, j], (yn, f))
 
-    own(0)
+    own_in()
+    own_y()
     for each in local[:2]:
         each.wait()
     hidT[...] = hid_ref[...].T
@@ -420,68 +438,80 @@
     def soon(has, s):
         return both_true(has, s >= first)
 
-    def behind(k):
-        if k == 0:
-            own(1)
-            return
-        for j in range(pieces[0]):
-            for way in (0, 1):
-                has, q, fwd = row(k, way)
-                s = q * 2 + y
-                under(both_true(has, s < first), relay, 0, s, fwd, j)
-        for way in (0, 1):
-            has, q, fwd = row(k, way)
-            under(has, relay, 1, q * 2 + y, fwd, 0)
-
     def ahead(k):
         for j in range(pieces[0]):
             for way in (0, 1):
                 has, q, fwd = row(k, way)
                 s = q * 2 + y
-                under(soon(has, s), relay, 0, s, fwd, j)
+                under(has, relay, s, fwd, j)
+                under(both_true(has, s >= first), cross, 0, s, j)
+
+    def cross_rest():
+        for k in range(1, outer):
+            for j in range(pieces[0]):
+                for way in (0, 1):
+                    has, q, _ = row(k, way)
+                    s = q * 2 + y
+                    under(both_true(has, s < first), cross, 0, s, j)
 
     def crossed(s):
         landed(0, s)
         take_in(s)
 
-    def run(steps, lags):
-        done = []
-
-        def trail(i):
-            for lag, name in zip(lags, ("pair_sum", "full_sum", "collect")):
-                if 0 <= i - lag < len(done):
-                    has, s, chain = done[i - lag]
-                    under(has, getattr(chain, name), s)
-
-        for has, fn, arg, chain in steps:
-            under(has, fn, arg)
-            if chain is not None:
-                done.append((has, arg, chain))
-                trail(len(done) - 1)
-
-        def rest():
-            for i in range(len(done), len(done) + lags[-1]):
-                trail(i)
-
-        return rest
-
-    steps = [(soon(None, c), take_in, c, ins), (None, ahead, 1, None)]
-    later = [(soon(None, yn), crossed, yn, ins)]
-    for k in range(1, outer):
-        if k > 1:
-            steps.append((None, ahead, k, None))
-        for way in (0, 1):
-            has, q, _ = row(k, way)
-            s = q * 2 + y
-            steps.append((soon(has, s), take_in, s, ins))
-        steps.extend(later)
-        steps.append((None, behind, k - 1, None))
-        later = []
-        for way in (0, 1):
-            has, q, _ = row(k, way)
-            s = q * 2 + 1 - y
-            later.append((soon(has, s), crossed, s, ins))
-    steps.extend(later)
+    items, at_stage, lags = [], [0, 0, 0], (3, 7, 11)
+    names = ("pair_sum", "full_sum", "collect")
+
+    def settle(stage, upto):
+        while at_stage[stage] < upto:
+            has, s, chain = items[at_stage[stage]]
+            under(has, getattr(chain, names[stage]), s)
+            at_stage[stage] += 1
+
+    def feed(has, fn, s, chain, push=True):
+        under(has, fn, s)
+        items.append((has, s, chain))
+        if push:
+            for stage, lag in enumerate(lags):
+                settle(stage, len(items) - lag)
+
+    def take_gate(s):
+        under(lax.rem(s + y, 2) != 0, landed, 0, s)
+        take_in(s)
+
+    def take_out(q):
+        for s in (q * 2, q * 2 + 1):
+            pl.when(q != z)(lambda s=s: landed(1, s))
+        at = pl.ds(pl.multiple_of(q * 2, 2), 2)
+        outs.take(q, dot1(wo_all[at].reshape(2 * rows_out, d), goutT[...], NN))
+
+    def plane(k):
+        for has, q in [(None, z)] if k == 0 else [row(k, way)[:2] for way in (0, 1)]:
+            for s in (q * 2, q * 2 + 1):
+                feed(both_true(has, s < first), take_gate, s, ins, False)
+            feed(has, take_out, q, outs, False)
+
+    def gather():
+        feed(soon(None, c), take_in, c, ins)
+        later = [(soon(None, yn), yn)]
+        for k in range(1, outer):
+            ahead(k)
+            if k == outer - 1:
+                cross_rest()
+                own_out()
+            for way in (0, 1):
+                has, q, _ = row(k, way)
+                feed(soon(has, q * 2 + y), take_in, q * 2 + y, ins)
+            for has, s in later:
+                feed(has, crossed, s, ins)
+            later = []
+            for way in (0, 1):
+                has, q, _ = row(k, way)
+                s = q * 2 + 1 - y
+                later.append((soon(has, s), s))
+        for has, s in later:
+            feed(has, crossed, s, ins)
+        for stage in range(3):
+            settle(stage, len(items))
 
     def decays():
         decay = dec_ref[...]
@@ -497,15 +527,16 @@
         e_out[...] = jnp.broadcast_to(
             e_ref[pl.ds(pl.multiple_of(f * hpf, 8), 8), tok - 128 : tok][:, 127:128], (8, nst))
         e_all[c] = e_out[...]
-        for k in range(1, n):
-            start(e_out, e_all.at[c], t_send.at[0], t_recv.at[0, c], (lax.rem(c + k, n), f))
-        total(e_all.at[pl.ds(0, n - 1)], e_all.at[pl.ds(0, n - 1)], t_send.at[0], t_recv.at[0, 0])
 
     for each in local[2:]:
         each.wait()
     goutT[...] = gout_ref[...].T
     decays()
-    run(steps, (2, 5, 8))()
+    gather()
+
+    for k in range(1, n):
+        start(e_out, e_all.at[c], t_send.at[0], t_recv.at[0, c], (lax.rem(c + k, n), f))
+    total(e_all.at[pl.ds(0, n - 1)], e_all.at[pl.ds(0, n - 1)], t_send.at[0], t_recv.at[0, 0])
 
     e = e_ref[...]
     einv = 1.0 / e
@@ -516,7 +547,7 @@
     xs2, b2, c2 = split(xs), split(bT), split(cT)
     tmp[...] = dot3(xs2, b2, NT) * eend
     own_rows = pl.ds(pl.multiple_of(f * hpf, 8), hpf)
-    st_out[...] = tmp[own_rows, :]
+    st_out[...] = tmp[own_rows, :].astype(bf16)
     for k in range(n - 1, 0, -1):
         go(st_out, st_all.at[c], s_send.at[0, k], s_recv.at[0, c],
            (jnp.minimum(c + k, n - 1), f), when=c + k < n)
@@ -525,44 +556,10 @@
         jnp.int32, (tok, tok), 1)
     scores2 = split(jnp.where(upper, dot3(transposed(b2), c2, NN), 0.0))
     y_in = dot3(xs2, scores2, NN)
-    behind(outer - 1)
-
-    def take_gate(s):
-        under(lax.rem(s + y, 2) != 0, landed, 0, s)
-        take_in(s)
-
-    def take_out(q):
-        landed(1, q * 2 + 1 - y)
-        at = pl.ds(pl.multiple_of(q * 2, 2), 2)
-        outs.take(q, dot1(wo_all[at].reshape(2 * rows_out, d), goutT[...], NN))
-
-    more = [(None, take_out, z, outs)]
-    for k in range(1, outer):
-        if k == outer - 1:
-            more.extend((None, take_gate, s, ins) for s in range(first))
-        for way in (0, 1):
-            has, q, _ = row(k, way)
-            more.append((has, take_out, q, outs))
-    rest = run(more, (2, 4, 6))
-
-    for k in range(1, n):
-        s = lax.rem(c + n - k, n)
-        copy(e_out, e_all.at[s], t_send.at[0], t_recv.at[0, s], (s, f)).wait_recv()
-        s = jnp.maximum(c - k, 0)
-        pl.when(c - k >= 0)(lambda s=s, k=k: copy(
-            st_out, st_all.at[s], s_send.at[0, k], s_recv.at[0, s], (s, f)).wait_recv())
-    state = jnp.zeros((hpf, nst), f32)
-    for k in range(n - 1):
-        new = e_all[k, 0:1, :] * state + st_all[k]
-        state = jnp.where(k < c, new, state)
-    s0_ref[own_rows, :] = state
-
     def share(ref, i):
         for k in range(1, fs):
             start(ref.at[own_rows], ref.at[own_rows], t_send.at[i], t_recv.at[i, f],
                   (c, lax.rem(f + k, fs)))
-        total(st_all.at[pl.ds(0, fs - 1)], st_all.at[pl.ds(0, fs - 1)], t_send.at[i],
-              t_recv.at[i, 0])
 
     def shared(ref, i):
         for k in range(1, fs):
@@ -570,15 +567,42 @@
             rows = pl.ds(pl.multiple_of(p * hpf, 8), hpf)
             copy(ref.at[rows], ref.at[rows], t_send.at[i], t_recv.at[i, p], (c, p)).wait_recv()
 
-    share(s0_ref, 1)
-    rest()
+    def start_state():
+        for k in range(1, n):
+            s = lax.rem(c + n - k, n)
+            copy(e_out, e_all.at[s], t_send.at[0], t_recv.at[0, s], (s, f)).wait_recv()
+            s = jnp.maximum(c - k, 0)
+            pl.when(c - k >= 0)(lambda s=s, k=k: copy(
+                st_out, st_all.at[s], s_send.at[0, k], s_recv.at[0, s], (s, f)).wait_recv())
+        state = jnp.zeros((hpf, nst), f32)
+        for k in range(n - 1):
+            new = e_all[k, 0:1, :] * state + st_all[k].astype(f32)
+            state = jnp.where(k < c, new, state)
+        s0_ref[own_rows, :] = state.astype(bf16)
+        share(s0_ref, 1)
+
+    for i in (1, 2):
+        some_f = st_all.at[pl.ds(0, fs - 1)]
+        total(some_f, some_f, t_send.at[i], t_recv.at[i, 0])
+    plane(0)
+    plane(1)
+    settle(0, len(items))
+    soonest = len(items)
+    for k in range(2, outer):
+        plane(k)
+    settle(0, len(items))
+    settle(1, soonest)
+    start_state()
+    settle(1, len(items))
+
+    settle(2, len(items))
     gate = pT[:hp, :]
     sig = 1.0 / (1.0 + jnp.exp(-gate))
     silu = gate * sig
 
     shared(s0_ref, 1)
-    s02 = split(s0_ref[...])
-    yT = (y_in + dot3(s02, c2, NN)) * e
+    s0 = s0_ref[...]
+    yT = (y_in + (dot1(s0, c2[0], NN) + dot1(s0, c2[1], NN))) * e
 
     gain = jnp.broadcast_to(gain_ref[...].reshape(1, hp), (8, hp)).T[:, 0:1]
     gated = yT * silu
@@ -593,18 +617,17 @@
         go(ad_out, ad_all.at[c], s_send.at[1, k], s_recv.at[1, c],
            (jnp.maximum(c - k, 0), f), when=c - k >= 0)
 
-    ro[...] = dot1(normed, gout_ref[...], NN)
-    for q in range(outer):
-        at = pl.ds(pl.multiple_of((q * 2 + 1 - y) * rows_out, 8), rows_out)
-        ob1[q] = ro[at, :].astype(bf16)
-    go(ob1, ob1r, o_send.at[0], o_recv.at[0], (yn, f))
-
-    blocks = [early[0] + late[0], early[1] + late[1]]
-    n_early, n_blocks = len(early[0]), len(blocks[0])
-
-    def pick(i, part, side):
-        a, b = blocks[0][i][part], blocks[1][i][part]
-        return a + side * (b - a)
+    blocks = [
+        [a + sorted(b, key=lambda block: block[1] if up_side else -block[1])
+         for a, b in zip(early, late)]
+        for up_side in (0, 1)
+    ]
+    n_gate = min(sum(b[0] + g <= hp for b in of_y) for of_y in early)
+    n_early, n_blocks = len(early[0]), len(blocks[0][0])
+
+    def pick(i, part, to):
+        (a, b), (p, q) = [[of_y[i][part] for of_y in of_side] for of_side in blocks]
+        return a + to * (b - a) + side * (p - a + to * (q - p - b + a))
 
     def to_partner(lo, hi):
         for i in range(lo, hi):
@@ -612,29 +635,79 @@
             ib1[i] = rin[at, :].astype(bf16)
             start(ib1.at[i], ib1r.at[i], i_send.at[0], iy_recv.at[i], (yn, f))
 
+    near = half - 1 + side
+    is_near = z == near
+
+    def place_of(i):
+        q, j = pick(i, 1, y), pick(i, 2, y)
+        return pl.ds(pl.multiple_of(pick(i, 0, y), 8), g), q, j, q // half != side
+
+    def onward(i, value, q, j):
+        ib2[i] = value.astype(bf16)
+        copy(ib2.at[i], ib2r.at[z, j], i_send.at[1], iz_recv.at[0], (q * 2 + y, f)).start()
+
+    def merge_one(i):
+        copy(ib1.at[i], ib1r.at[i], i_send.at[0], iy_recv.at[i], (yn, f)).wait_recv()
+        at, q, j, cross = place_of(i)
+        value = rin[at, :] + ib1r[i].astype(f32)
+
+        def keep():
+            ri[pl.ds(pl.multiple_of(j * g, 8), g), :] = value
+
+        def hold():
+            rin[at, :] = value
+
+        def hand():
+            ib2[i] = value.astype(bf16)
+            slot = z - side * (half + 1)
+            copy(ib2.at[i], irx.at[slot, i], i_send.at[1], ir_recv.at[slot, i],
+                 (near * 2 + y, f)).start()
+
+        stay = jnp.logical_not(cross)
+        pl.when(q == z)(keep)
+        pl.when(jnp.logical_and(stay, q != z))(lambda: onward(i, value, q, j))
+        pl.when(jnp.logical_and(cross, is_near))(hold)
+        if half > 1:
+            pl.when(jnp.logical_and(cross, jnp.logical_not(is_near)))(hand)
+
+    def cross_one(i):
+        at, q, j, cross = place_of(i)
+
+        def add():
+            value = rin[at, :]
+            for slot in range(half - 1):
+                copy(ib2.at[i], irx.at[slot, i], i_send.at[1], ir_recv.at[slot, i],
+                     (yn, f)).wait_recv()
+                value = value + irx[slot, i].astype(f32)
+            onward(i, value, q, j)
+
+        pl.when(jnp.logical_and(cross, is_near))(add)
+
     def merge(lo, hi):
         for i in range(lo, hi):
-            copy(ib1.at[i], ib1r.at[i], i_send.at[0], iy_recv.at[i], (yn, f)).wait_recv()
-            at = pl.ds(pl.multiple_of(pick(i, 0, y), 8), g)
-            value = rin[at, :] + ib1r[i].astype(f32)
-            q, j = pick(i, 1, y), pick(i, 2, y)
-
-            def keep():
-                ri[pl.ds(pl.multiple_of(j * g, 8), g), :] = value
-
-            def send():
-                ib2[i] = value.astype(bf16)
-                copy(ib2.at[i], ib2r.at[z, j], i_send.at[1], iz_recv.at[0], (q * 2 + y, f)).start()
-
-            pl.when(q == z)(keep)
-            pl.when(q != z)(send)
-
-    dscores = jnp.where(upper, dot1(xs2[0].T, dys2[0], NN), 0.0).astype(bf16)
+            merge_one(i)
+            if i >= 3:
+                cross_one(i - 3)
+        if hi == n_blocks:
+            for i in range(max(hi - 3, 0), hi):
+                cross_one(i)
+
     gp[:hp, :] = (dgated * yT * (sig * (1.0 + gate * (1.0 - sig)))).astype(bf16)
     rin[:hp, :] = dot1(gp[:hp, :], hid_ref[...], NN)
-    gp[2 * hp + nst :, :] = (dot1(b2[0], dscores, NN) + dot3(transposed(s02), dys2, NN)).astype(bf16)
+    to_partner(0, n_gate)
+    ro[...] = dot1(normed, gout_ref[...], NN)
+    for q in range(outer):
+        ob1[q] = ro[q * 2 * rows_out : (q + 1) * 2 * rows_out, :].astype(bf16)
+    for k in range(outer - 1, 0, -1):
+        q = lax.rem(z + k, outer)
+        start(ob1.at[q], ob1r.at[z], o_send.at[0], o_recv.at[0], (q * 2 + y, f))
+    some = pl.ds(0, outer - 1)
+    total(ob1.at[some], ob1r.at[some], o_send.at[0], o_recv.at[0])
+
+    dscores = jnp.where(upper, dot1(xs2[0].T, dys2[0], NN), 0.0).astype(bf16)
+    gp[2 * hp + nst :, :] = (dot1(b2[0], dscores, NN) + dot1(s0.T, dys2[0], NN)).astype(bf16)
     rin[2 * hp + nst :, :] = dot1(gp[2 * hp + nst :, :], hid_ref[...], NN)
-    to_partner(0, n_early)
+    to_partner(n_gate, n_early)
     db = dot1(c2[0], dscores, NT)
     dxs = dot1(dys2[0], scores2[0], NT)
 
@@ -646,24 +719,12 @@
     for k in range(n - 1, 0, -1):
         new = e_all[k, 0:1, :] * adj + ad_all[k].astype(f32)
         adj = jnp.where(k > c, new, adj)
-    g_ref[own_rows, :] = adj
+    g_ref[own_rows, :] = adj.astype(bf16)
     share(g_ref, 2)
-
-    copy(ob1, ob1r, o_send.at[0], o_recv.at[0], (yn, f)).wait_recv()
-    for q in range(outer):
-        at = pl.ds(pl.multiple_of((q * 2 + y) * rows_out, 8), rows_out)
-        value = ro[at, :] + ob1r[q].astype(f32)
-        ro[at, :] = value
-        ob2[q] = value.astype(bf16)
-    for k in range(1, outer):
-        q = lax.rem(z + k, outer)
-        start(ob2.at[q], ob2r.at[z], o_send.at[1], o_recv.at[1], (q * 2 + y, f))
-    some = pl.ds(0, outer - 1)
-    total(ob2.at[some], ob2r.at[some], o_send.at[1], o_recv.at[1])
 
     merge(0, 2)
     shared(g_ref, 2)
-    g2 = split(g_ref[...] * eend)
+    g2 = split(g_ref[...].astype(f32) * eend)
     gp[hp : 2 * hp, :] = ((dxs + dot3(g2, b2, NN)) * einv).astype(bf16)
     gp[2 * hp : 2 * hp + nst, :] = (db + dot3(transposed(g2), xs2, NN)).astype(bf16)
     rin[hp : 2 * hp + nst, :] = dot1(gp[hp : 2 * hp + nst, :], hid_ref[...], NN)
@@ -671,24 +732,24 @@
     total(ib1, ib1r, i_send.at[0], iy_recv.at[0])
     merge(2, n_early)
 
-    gpt = gp[...].T
-    wi = wi_all[...].reshape(cin, d)
-    gh_ref[...] = dot1(gpt, wi, NN).astype(bf16)
-    put_gh = pltpu.make_async_copy(gh_ref, gh_any, l_sem.at[6])
-    put_gh.start()
-
-    weight = jnp.zeros((1, d), f32)
-    for s in range(n):
-        w = wo_all[s].astype(f32)
-        weight = weight + jnp.sum(w * w, axis=0, keepdims=True)
-    w = wi_all[c].astype(f32)
-    weight_in = jnp.sum(w * w, axis=1, keepdims=True)
-
-    copy(ob2.at[some], ob2r.at[some], o_send.at[1], o_recv.at[1], (yn, f)).wait_recv()
-    acc = ro[pl.ds(pl.multiple_of(c * rows_out, 8), rows_out), :]
-    for k in range(1, outer):
-        q = lax.rem(z + k, outer)
-        acc = acc + ob2r[q].astype(f32)
+    late_on = max(n_blocks - 3, n_early)
+    merge(n_early, late_on)
+    copy(ob1.at[some], ob1r.at[some], o_send.at[0], o_recv.at[0], (yn, f)).wait_recv()
+
+    def plane_sum(side_y):
+        at = pl.ds(pl.multiple_of((z * 2 + side_y) * rows_out, 8), rows_out)
+        from_y = pl.ds(pl.multiple_of(side_y * rows_out, 8), rows_out)
+        value = ro[at, :]
+        for k in range(1, outer):
+            value = value + ob1r[lax.rem(z + k, outer), from_y, :].astype(f32)
+        return value
+
+    ob2[...] = plane_sum(1 - y).astype(bf16)
+    go(ob2, ob2r, o_send.at[1], o_recv.at[1], (yn, f))
+    out_part = plane_sum(y)
+    merge(late_on, n_blocks)
+    copy(ob2, ob2r, o_send.at[1], o_recv.at[1], (yn, f)).wait_recv()
+    acc = out_part + ob2r[...].astype(f32)
     acc = acc * (1.0 / root_tokens)
     ro[:rows_out, :] = acc
     nout_out[...] = jnp.sum(acc * acc, axis=0, keepdims=True).reshape(8, d // 8)
@@ -697,16 +758,30 @@
     total(nout_all.at[pl.ds(0, n - 1)], nout_all.at[pl.ds(0, n - 1)], n_send.at[0], n_recv.at[0, 0])
     nout_all[c] = nout_out[...]
 
-    merge(n_early, n_blocks)
     sent = n_blocks - rows_in // g
     most = pl.ds(0, sent)
     total(ib2.at[most], ib2.at[most], i_send.at[1], iz_recv.at[0])
 
-    copy(ib2r.at[some], ib2r.at[some], i_send.at[1], iz_recv.at[0], (yn, f)).wait_recv()
+    gpt = gp[...].T
+    wi = wi_all[...].reshape(cin, d)
+    gh_ref[...] = dot1(gpt, wi, NN).astype(bf16)
+    put_gh = pltpu.make_async_copy(gh_ref, gh_any, l_sem.at[6])
+    put_gh.start()
+
+    weight = jnp.zeros((1, d), f32)
+    for s in range(n):
+        w = wo_all[s].astype(f32)
+        weight = weight + jnp.sum(w * w, axis=0, keepdims=True)
+    w = wi_all[c].astype(f32)
+    weight_in = jnp.sum(w * w, axis=1, keepdims=True)
+
+    full = ib2r.at[pl.ds(0, half)]
+    copy(full, full, i_send.at[1], iz_recv.at[0], (yn, f)).wait_recv()
     acc = ri[...]
-    for k in range(1, outer):
-        q = lax.rem(z + k, outer)
+    for k in range(1, half):
+        q = side * half + lax.rem(z - side * half + k, half)
         acc = acc + ib2r[q].reshape(rows_in, d).astype(f32)
+    acc = acc + ib2r[half - side].reshape(rows_in, d).astype(f32)
     acc = acc * (1.0 / root_tokens)
     ri[...] = acc
     at = lax.broadcasted_iota(jnp.int32, (rows_in, 128), 1)
@@ -743,21 +818,35 @@
 
     ins.finish()
     outs.finish()
-    for a, (_, ref) in enumerate(both):
-        for at in range(outer):
-            if at < outer - 1:
-                part = ref.at[pl.ds(0, at + 1)]
-                total(part, part, g_send.at[0, a], g_recv.at[a, 0], z == at)
-            if at > 0:
-                part = ref.at[pl.ds(0, outer - at)]
-                total(part, part, g_send.at[1, a], g_recv.at[a, 0], z == at)
-        part = ref.at[pl.ds(0, outer)]
-        total(part, part, g_send.at[2, a], g_recv.at[a, 0])
+    for at in range(outer):
+        if at < outer - 1:
+            part_up = wi_all.at[pl.ds(0, at + 1)]
+            total(part_up, part_up, g_send.at[0, 0], g_recv.at[0, 0, 0], z == at)
+        if at > 0:
+            part_down = wi_all.at[pl.ds(0, outer - at)]
+            total(part_down, part_down, g_send.at[1, 0], g_recv.at[0, 0, 0], z == at)
+    part_y = wi_all.at[pl.ds(0, outer)]
+    total(part_y, part_y, g_send.at[2, 0], g_recv.at[0, 0, 0])
+    part_z = wo_all.at[pl.ds(0, outer - 1)]
+    for way in (0, 1):
+        total(part_z, part_z, g_send.at[way, 1], g_recv.at[1, 0, 0])
+    total(wo_all.at[0], wo_all.at[0], g_send.at[2, 1], g_recv.at[1, 0, 0])
     for has, args in ends:
         under(has, lambda args=args: copy(*args).wait_send())
     put_gh.wait()
     put_gwo.wait()
     put_gwi.wait()
+
+
+def write_out(a_ref, b_ref, c_ref, ao_ref, bo_ref, co_ref, sem):
+    copies = [
+        pltpu.make_async_copy(src, dst, sem.at[i])
+        for i, (src, dst) in enumerate(((a_ref, ao_ref), (b_ref, bo_ref), (c_ref, co_ref)))
+    ]
+    for each in copies:
+        each.start()
+    for each in copies:
+        each.wait()
 
 
 def one_kernel(n, fs, hidden, w_in, decay, norm_gain, w_out, grad_out):
@@ -780,23 +869,25 @@
         V((outer, rows_out, tok), bf16), V((outer, rows_out, tok), bf16),
         V((outer, rows_out, tok), f32),
         V((8, nst), f32), V((n, 8, nst), f32),
-        V((hp, tok), f32), V((hpf, nst), f32), V((n, hpf, nst), f32), V((hp, nst), f32),
-        V((hpf, nst), bf16), V((n, hpf, nst), bf16), V((hp, nst), f32),
-        V((hp, d), f32), V((outer, rows_out, d), bf16), V((outer, rows_out, d), bf16),
-        V((outer, rows_out, d), bf16), V((outer, rows_out, d), bf16),
+        V((hp, tok), f32), V((hpf, nst), bf16), V((n, hpf, nst), bf16), V((hp, nst), bf16),
+        V((hpf, nst), bf16), V((n, hpf, nst), bf16), V((hp, nst), bf16),
+        V((hp, d), f32), V((outer, 2 * rows_out, d), bf16), V((outer, 2 * rows_out, d), bf16),
+        V((rows_out, d), bf16), V((rows_out, d), bf16),
         V((cin, tok), bf16), V((cin, d), f32), V((rows_in, d), f32),
         V((blocks, g, d), bf16), V((blocks, g, d), bf16),
         V((blocks, g, d), bf16), V((outer, per, g, d), bf16),
+        V((max(outer // 2 - 1, 1), blocks, g, d), bf16),
         V((16, rows_in), f32), V((fs, 16, rows_in), f32),
         V((8, d // 8), f32), V((n, 8, d // 8), f32),
         dma((3, 2)), dma((2, n, per)), dma((3,)), dma((3, n)), dma((3,)), dma((3, outer)),
         dma((2, n)), dma((2, n)), dma((3,)), dma((3, n)),
         dma((2,)), dma((2,)), dma((2,)), dma((blocks,)), dma((1,)),
+        dma((max(outer // 2 - 1, 1), blocks)),
         dma((2,)), dma((2, n)), V((hp, nst), f32),
         V((tok, d), bf16), V((tok, d), bf16), V(decay.shape, f32), V((hp,), f32),
         V((tok, d), bf16), V((rows_in, d), f32), V((rows_out, d), f32), dma((9,)),
     ]
-    return pl.pallas_call(
+    outs = pl.pallas_call(
         functools.partial(fused, n, fs, math.sqrt(tok * n), math.sqrt(d * fs)),
         out_shape=(
             V((tok, d), bf16),
@@ -809,6 +900,13 @@
         compiler_params=pltpu.CompilerParams(
             collective_id=0, has_side_effects=True, vmem_limit_bytes=60 * 1024 * 1024),
     )(hidden, w_in, decay, norm_gain, w_out, grad_out)
+    return pl.pallas_call(
+        write_out,
+        out_shape=tuple(jax.ShapeDtypeStruct(o.shape, o.dtype) for o in outs),
+        in_specs=[pl.BlockSpec(memory_space=pltpu.VMEM)] * 3,
+        out_specs=(pl.BlockSpec(memory_space=pl.ANY),) * 3,
+        scratch_shapes=[dma((3,))],
+    )(*[pltpu.with_memory_space_constraint(o, pltpu.VMEM) for o in outs])
 
 
 def solution(mesh):

time: 90.1 us -> 74.7 us (0.83)
  the two profiles are of different devices: /device:TPU:25 before, /device:TPU:0 now
where the time goes in v3:
time: 74.7 us; the launch traced here: 73.5 us
  Pallas kernels  72.7 us (97%)
  between operations  0.8 us (1%)
    pallas_call x1, Pallas kernels, one_kernel(): pl.pallas_call(functools.partial(fused, n, fs, math.sqrt(tok * n), math.s...  71.6 us

profile of v3, /device:TPU:0, one launch (start us, length us, event | category | flops | bytes accessed | tf_op | source)
XLA Modules:
  0.0 73.5 jit_solution(8501616713547044592)
XLA Ops:
  0.6 71.6 %shard_map.85 = (bf16[512,1024]{1,0:T(8,128)(2,1)S(1)}, f32[96,1024]{1,0:T(8,128)S(1)}, f32[32,1024]{1,0:T(8,128)S(1)}) custom-call(bf16[512,1024]{1,0:T(8,128)(2,1)} %hid_any.1, bf16[96,1024]{1,0:T(8,128)(2,1)} %win_ref.1, f32[4,512]{1,0:T(4,128)} %dec_any.1, f32[256]{0:T(256)} %gain_any.1, bf16[32,1024]{1,0:T(8,128)(2,1)} %wout_ref.1, ...), custom_call_target="tpu_custom_call" | custom-call | tf_op jit(solution)/shard_map/pallas_call | solution.py:890
  72.2 1.2 %shard_map.86 = (bf16[512,1024]{1,0:T(8,128)(2,1)}, f32[96,1024]{1,0:T(8,128)}, f32[32,1024]{1,0:T(8,128)}) custom-call(bf16[512,1024]{1,0:T(8,128)(2,1)S(1)} %get-tuple-element.6.a_ref, f32[96,1024]{1,0:T(8,128)S(1)} %get-tuple-element.7.b_ref, f32[32,1024]{1,0:T(8,128)S(1)} %get-tuple-element.8.c_ref), custom_call_target="tpu_custom_call" | custom-call | tf_op jit(solution)/shard_map/pallas_call | solution.py:903
